TPU v7x, 256 devices: a whole 4x4x8 slice. The times are simulated.
256 devices in a mesh: dp: 2 (over z_lo), ctx: 32 (over z_hi, y, core), tensor: 4 (over x).
Axes of the slice: x: 4, y: 4, z: 8 (z_hi: 4, z_lo: 2; z = z_hi * 2 + z_lo), core: 2. Of those that a mesh axis runs over, the one named last changes fastest.
Arguments:
- queries: bfloat16 [8192, 3072], P(('dp', 'ctx'), 'tensor'), parts along dimension 0, may hold values from -6 to 6
- keys: bfloat16 [8192, 512], P(('dp', 'ctx'), 'tensor'), parts along dimension 0, may hold values from -6 to 6
- values: bfloat16 [8192, 512], P(('dp', 'ctx'), 'tensor'), parts along dimension 0, may hold values from -6 to 6
- cache_keys: bfloat16 [8192, 512], P(('dp', 'ctx'), 'tensor'), parts along dimension 0, may hold values from -6 to 6
- cache_values: bfloat16 [8192, 512], P(('dp', 'ctx'), 'tensor'), parts along dimension 0, may hold values from -6 to 6
- residual: bfloat16 [8192, 3072], P(('dp', 'ctx'), 'tensor'), parts along dimension 0, may hold values from -36 to 36
- norm_gain: float32 [3072], replicated, may hold values from 0.1 to 1.9
- w_gate: bfloat16 [3072, 65536], P(None, ('ctx', 'tensor')), may hold values from -0.109375 to 0.109375
- w_up: bfloat16 [3072, 65536], P(None, ('ctx', 'tensor')), may hold values from -0.109375 to 0.109375
- w_down: bfloat16 [65536, 3072], P(('ctx', 'tensor')), may hold values from -0.0625 to 0.0625
- expert_ids: int32 [8192, 2], P(('dp', 'ctx')), parts along dimension 0, may hold values from 0 to 7, all different within a row; in each aligned block of 128 rows (0 to 127, 128 to 255, ...) at most 36 rows name the same one
- gate_weights: float32 [8192, 2], P(('dp', 'ctx')), parts along dimension 0, may hold values from 0.1 to 0.9
Outputs:
- layer_out: bfloat16 [8192, 3072], P(('dp', 'ctx'), 'tensor'), parts along dimension 0
There are 2 independent parts, one for each index of `dp`. A program takes and returns all parts, laid end to end along the dimension named above; an argument that names none is the same for every part. Nothing has to cross between parts.
Inputs may be any that keep to these rules, and one draw needn't show every extreme that they name: `expert_ids`: among the 128 rows of each index of ctx (aligned blocks of rows), no expert is named by more than 36 rows, a bound that some block reaches.
All inputs are finite; a program needn't handle non-finite values.
Results may differ from a plain program's by a relative error of at most 0.012.
Values may be sent and summed in bfloat16 or wider, within the bound.
No kernel may reach another device: no remote copies, remote signals or barrier semaphores. Data moves between devices by JAX's collectives and lax.ppermute only.
A program may use at most 192 MiB of HBM per device.

v0:
```python
import math

import jax
import jax.numpy as jnp
from jax import lax
from jax.sharding import PartitionSpec as P

HEADS = 24
KV_HEADS = 4
HEAD_DIM = 128
EXPERTS = 8
TOP = 2
CAP = 36


eps = 1e-05
neg_big = -1e30


def attend_block(
    carried, query_heads, key_block, value_block, key_pos, query_pos, window, score_scale
):
    run_max, run_sum, accumulated = carried
    scores = (
        jnp.einsum("qkgd,tkd->kgqt", query_heads, key_block, preferred_element_type=jnp.float32)
        * score_scale
    )
    allowed = (key_pos[None, :] <= query_pos[:, None]) & (
        key_pos[None, :] > query_pos[:, None] - window
    )
    scores = jnp.where(allowed[None, None], scores, neg_big)
    new_max = jnp.maximum(run_max, jnp.max(scores, axis=-1))
    weights = jnp.where(allowed[None, None], jnp.exp(scores - new_max[..., None]), 0.0)
    run_sum = jnp.sum(weights, axis=-1)
    update = jnp.einsum(
        "kgqt,tkd->kgqd",
        weights.astype(jnp.bfloat16),
        value_block,
        preferred_element_type=jnp.float32,
    )
    accumulated = update
    return (new_max, run_sum, accumulated)


def expert_block(full_rows, norm_gain, w_gate, w_up, w_down):
    widened = full_rows.astype(jnp.float32)
    inverse = lax.rsqrt(jnp.mean(widened * widened, axis=-1, keepdims=True) + eps)
    normed = (widened * inverse * norm_gain).astype(jnp.bfloat16)
    gate_proj = jnp.dot(normed, w_gate, preferred_element_type=jnp.float32)
    up_proj = jnp.dot(normed, w_up, preferred_element_type=jnp.float32)
    activated = (jax.nn.silu(gate_proj) * up_proj).astype(jnp.bfloat16)
    return jnp.dot(activated, w_down, preferred_element_type=jnp.float32)


def route_tables(expert_ids, gate_weights):
    tok_rows = expert_ids.shape[0]
    flat_ids = expert_ids.reshape(-1)
    member = (flat_ids[:, None] == jnp.arange(EXPERTS, dtype=jnp.int32)[None, :]).astype(jnp.int32)
    earlier = jnp.cumsum(member, axis=0) - member
    rank_in = jnp.sum(earlier * member, axis=1)
    slot_of = flat_ids * CAP + rank_in
    picks = (jnp.arange(EXPERTS * CAP, dtype=jnp.int32)[:, None] == slot_of[None, :]).astype(
        jnp.float32
    )
    select = jnp.sum(picks.reshape(EXPERTS * CAP, tok_rows, TOP), axis=2).astype(jnp.bfloat16)
    weighing = jnp.sum(
        (picks * gate_weights.reshape(-1)[None, :]).reshape(EXPERTS * CAP, tok_rows, TOP), axis=2
    )
    return (select, weighing)


def per_device(
    queries,
    keys,
    values,
    cache_keys,
    cache_values,
    residual,
    norm_gain,
    w_gate,
    w_up,
    w_down,
    expert_ids,
    gate_weights,
):
    tok_rows = queries.shape[0]
    n_ctx = lax.axis_size("ctx")
    n_tensor = lax.axis_size("tensor")
    window = tok_rows * n_ctx
    kv_local = keys.shape[1] // HEAD_DIM
    group_size = HEADS // KV_HEADS
    score_scale = 1.0 / math.sqrt(HEAD_DIM)
    query_heads = queries.reshape(tok_rows, kv_local, group_size, HEAD_DIM)
    my_index = lax.axis_index("ctx")
    query_pos = my_index * tok_rows + jnp.arange(tok_rows, dtype=jnp.int32)
    initial = (
        jnp.full((kv_local, group_size, tok_rows), neg_big, jnp.float32),
        jnp.zeros((kv_local, group_size, tok_rows), jnp.float32),
        jnp.zeros((kv_local, group_size, tok_rows, HEAD_DIM), jnp.float32),
    )
    stacked = jnp.stack((cache_keys, cache_values, keys, values))
    shard_piece = lax.all_gather(stacked, "ctx", axis=1, tiled=True)
    span_rows = shard_piece.shape[1]
    offsets = jnp.arange(span_rows, dtype=jnp.int32)
    key_block = jnp.concatenate((shard_piece[0], shard_piece[2]), axis=0).reshape(
        2 * span_rows, kv_local, HEAD_DIM
    )
    value_block = jnp.concatenate((shard_piece[1], shard_piece[3]), axis=0).reshape(
        2 * span_rows, kv_local, HEAD_DIM
    )
    key_pos = jnp.concatenate((offsets - window, offsets))
    run_max, run_sum, accumulated = attend_block(
        initial, query_heads, key_block, value_block, key_pos, query_pos, window, score_scale
    )
    attended = (
        (accumulated / run_sum[..., None])
        .transpose(2, 0, 1, 3)
        .reshape(tok_rows, kv_local * group_size * HEAD_DIM)
    )
    hidden_state = (residual.astype(jnp.float32) + attended).astype(jnp.bfloat16)
    select, weighing = route_tables(expert_ids, gate_weights)
    quarter = hidden_state.shape[1]
    buffer = (
        jnp.dot(select, hidden_state, preferred_element_type=jnp.float32)
        .astype(jnp.bfloat16)
        .reshape(EXPERTS, CAP, quarter)
    )
    per_expert = n_ctx * n_tensor // EXPERTS
    outgoing = jnp.repeat(buffer, per_expert, axis=0)
    arrived = lax.all_to_all(outgoing, ("ctx", "tensor"), split_axis=0, concat_axis=2, tiled=True)
    item_count = arrived.shape[1]
    full_rows = arrived.reshape(item_count * n_ctx, n_tensor * quarter)
    partial_value = expert_block(full_rows, norm_gain, w_gate, w_up, w_down)
    gathered_parts = lax.all_to_all(
        partial_value.reshape(item_count, n_ctx * n_tensor, quarter).astype(jnp.bfloat16),
        ("ctx", "tensor"),
        split_axis=1,
        concat_axis=1,
        tiled=True,
    ).astype(jnp.float32)
    expert_out = (
        jnp.sum(gathered_parts.reshape(CAP, EXPERTS, per_expert, quarter), axis=2)
        .transpose(1, 0, 2)
        .reshape(EXPERTS * CAP, quarter)
    )
    mixture = lax.dot_general(
        weighing,
        expert_out,
        (((0,), (0,)), ((), ())),
        precision=lax.Precision.HIGHEST,
        preferred_element_type=jnp.float32,
    )
    return (hidden_state.astype(jnp.float32) + mixture).astype(jnp.bfloat16)


def solution(mesh):
    in_specs = (
        P(("dp", "ctx"), "tensor"),
        P(("dp", "ctx"), "tensor"),
        P(("dp", "ctx"), "tensor"),
        P(("dp", "ctx"), "tensor"),
        P(("dp", "ctx"), "tensor"),
        P(("dp", "ctx"), "tensor"),
        P(),
        P(None, ("ctx", "tensor")),
        P(None, ("ctx", "tensor")),
        P(("ctx", "tensor"), None),
        P(("dp", "ctx"), None),
        P(("dp", "ctx"), None),
    )
    out_specs = P(("dp", "ctx"), "tensor")
    return jax.shard_map(
        per_device, mesh=mesh, in_specs=in_specs, out_specs=out_specs, check_vma=False
    )
```

profile of v0, /device:TPU:32, one launch (start us, length us, event | category | flops | bytes accessed | tf_op | source)
XLA Modules:
  0.0 617.0 jit_solution(5046068293215143510)
XLA Ops:
  6.5 0.0 copy-start
  6.5 0.0 all-gather.2.cloned.1.call-start
  6.5 1.6 pad_maximum_fusion
  8.2 0.0 all-gather.2.cloned.1.call-update
  8.2 0.8 copy.79
  9.0 0.1 eq.45
  9.1 0.1 eq.41
  9.3 0.6 reduce-window.6
  9.9 0.2 slice_reduce_fusion
  10.1 0.1 fusion.20
  10.2 0.1 reduce_sum.67
  10.4 0.1 copy.81
  10.4 1.1 copy.74
  11.6 0.7 multiply_add_fusion
  12.3 1.5 convert_reduce_fusion.1
  13.7 4.4 compare_and_fusion
  18.2 53.7 %all-gather.2.cloned.1.call-done = bf16[4,4096,128]{2,1,0:T(8,128)(2,1)} async-done(((bf16[4,128,128]{2,1,0:T(8,128)(2,1)}), bf16[4,4096,128]{2,1,0:T(8,128)(2,1)}) %all-gather.2.cloned.1.call-update) | async-done | bytes 4194320 | tf_op jit(solution)/shard_map/all_gather | solution.py:102
  71.9 0.0 copy-start.2
  71.9 2.5 slice_bitcast_fusion.3
  74.5 0.0 copy-done.2
  74.5 14.3 %fusion = (f32[6,128]{1,0:T(8,128)S(1)}, f32[8192,128,6]{1,0,2:T(8,128)}) fusion(pred[128,8192]{0,1:T(8,128)(4,1)S(1)} %copy-done.2, bf16[128,6,128]{0,2,1:T(8,128)(2,1)S(1)} %bitcast.82, bf16[4096,128]{1,0:T(8,128)(2,1)S(1)} %get-tuple-element.10, bf16[4096,128]{1,0:T(8,128)(2,1)S(1)} %get-tuple-element.7), kind=kOutput, calls=%fused_computation.2 | convolution fusion | flops 1633680640 | bytes 28511232 | tf_op jit(solution)/shard_map/qkgd,tkd->kgqt/dot_general | solution.py:25
  88.8 11.4 %fusion.1 = f32[6,128]{1,0:T(8,128)S(1)} fusion(f32[8192,128,6]{1,0,2:T(8,128)} %get-tuple-element.12, f32[6,128]{1,0:T(8,128)S(1)} %broadcast_maximum_fusion, pred[128,8192]{0,1:T(8,128)(4,1)S(1)} %copy-done.2), kind=kLoop, calls=%fused_computation.5 | loop fusion | flops 31456512 | bytes 26220544 | tf_op jit(solution)/shard_map/reduce_sum | solution.py:34
  100.2 26.0 %fusion.15 = f32[6,128,128]{1,2,0:T(8,128)} fusion(bf16[4096,128]{1,0:T(8,128)(2,1)S(1)} %get-tuple-element.8, bf16[4096,128]{1,0:T(8,128)(2,1)S(1)} %get-tuple-element.9, f32[8192,128,6]{1,0,2:T(8,128)} %get-tuple-element.12, f32[6,128]{1,0:T(8,128)S(1)} %broadcast_maximum_fusion, pred[128,8192]{0,1:T(8,128)(4,1)S(1)} %copy-done.2, f32[6,128]{1,0:T(8,128)S(1)} %fusion.1), kind=kOutput, calls=%fused_computation.31 | convolution fusion | flops 1646362624 | bytes 28710912 | tf_op jit(solution)/shard_map/kgqt,tkd->kgqd/dot_general | solution.py:35
  126.2 1.2 copy.78
  127.4 2.0 convolution_convert_fusion.1
  129.4 1.9 reshape.190
  131.2 1.5 broadcast_in_dim.41
  132.8 188.8 %all_to_all.14 = bf16[128,36,768]{2,1,0:T(8,128)(2,1)S(1)} all-to-all(bf16[128,36,768]{2,1,0:T(8,128)(2,1)S(1)} %bitcast.78), channel_id=1, replica_groups=mesh['dp'=2,'ctx'=32,'tensor'=4] {'ctx','tensor'}, dimensions={0} | all-to-all | bytes 14155776 | tf_op jit(solution)/shard_map/all_to_all | solution.py:130
  321.6 0.0 copy-start.1
  321.6 3.1 copy-done.1
  324.7 2.3 fusion.3
  327.0 1.5 copy.83
  328.5 2.1 reduce_sum.72
  330.7 1.3 reduce_sum.73
  332.0 10.0 %convert_bitcast_fusion = f32[1,36,128,768]{3,1,2,0:T(8,128)} fusion(bf16[128,36,768]{2,1,0:T(8,128)(2,1)} %copy-done.1), kind=kLoop, calls=%fused_computation.4 | loop fusion | flops 3538944 | bytes 21233664 | tf_op jit(solution)/shard_map/convert_element_type | solution.py:46
  342.0 15.0 %copy.82 = f32[1,36,128,768]{3,2,1,0:T(8,128)} copy(f32[1,36,128,768]{3,1,2,0:T(8,128)} %convert_bitcast_fusion) | data formatting | bytes 28311552 | tf_op jit(solution)/shard_map/convert_element_type | solution.py:46
  357.0 16.7 %reshape.195 = f32[1152,3072]{1,0:T(8,128)} reshape(f32[1,36,128,768]{3,2,1,0:T(8,128)} %copy.82) | data formatting | bytes 28311552 | tf_op jit(solution)/shard_map/convert_element_type | solution.py:46
  373.6 11.3 %fusion.28 = f32[1152,512]{1,0:T(8,128)} fusion(bf16[3072,512]{1,0:T(8,128)(2,1)} %param.19, f32[1152,3072]{1,0:T(8,128)} %reshape.195, f32[3072]{0:T(1024)} %param.18, f32[1152]{0:T(1024)S(1)} %add_rsqrt_fusion), kind=kOutput, calls=%fused_computation.58 | convolution fusion | flops 3634495488 | bytes 19677696 | tf_op jit(solution)/shard_map/dot_general | solution.py:49
  384.9 0.0 copy-done
  384.9 14.3 %convolution_convert_fusion = bf16[1152,3072]{1,0:T(8,128)(2,1)} fusion(bf16[512,3072]{1,0:T(8,128)(2,1)S(1)} %copy-done, bf16[3072,512]{1,0:T(8,128)(2,1)} %param.20, f32[1152,512]{1,0:T(8,128)} %fusion.28, f32[1152,3072]{1,0:T(8,128)} %reshape.195, f32[3072]{0:T(1024)} %param.18, f32[1152]{0:T(1024)S(1)} %add_rsqrt_fusion), kind=kOutput, calls=%fused_computation.13 | convolution fusion | flops 7265452032 | bytes 29901312 | tf_op jit(solution)/shard_map/dot_general | solution.py:52
  399.2 11.9 %convert_element_type.79 = bf16[36,128,768]{2,1,0:T(8,128)(2,1)} reshape(bf16[1152,3072]{1,0:T(8,128)(2,1)} %convolution_convert_fusion) | data formatting | bytes 14155776 | tf_op jit(solution)/shard_map/convert_element_type | solution.py:135
  411.2 7.0 %copy.84 = bf16[36,128,768]{2,0,1:T(8,128)(2,1)S(1)} copy(bf16[36,128,768]{2,1,0:T(8,128)(2,1)} %convert_element_type.79) | data formatting | bytes 14155776 | tf_op jit(solution)/shard_map/convert_element_type | solution.py:135
  418.2 184.5 %all_to_all.15 = bf16[36,128,768]{2,0,1:T(8,128)(2,1)S(1)} all-to-all(bf16[36,128,768]{2,0,1:T(8,128)(2,1)S(1)} %copy.84), channel_id=1, replica_groups=mesh['dp'=2,'ctx'=32,'tensor'=4] {'ctx','tensor'}, dimensions={1} | all-to-all | bytes 14155776 | tf_op jit(solution)/shard_map/all_to_all | solution.py:134
  602.7 2.1 convert_reduce_fusion
  604.8 2.2 reshape.194
  607.0 2.7 fusion.14
  (9 shorter events, 0.1 us)
Async XLA Ops:
  6.5 378.4 %copy-start = (bf16[512,3072]{1,0:T(8,128)(2,1)S(1)}, bf16[512,3072]{1,0:T(8,128)(2,1)}, u32[]{:S(2)}) copy-start(bf16[512,3072]{1,0:T(8,128)(2,1)} %param.21) | copy-start | bytes 9437188
  6.5 65.4 %all-gather.2.cloned.1.call-start = ((), (), s32[]{:S(2)}) async-start(), calls=%async_computation.2 | async-start | bytes 4325376 | tf_op jit(solution)/shard_map/all_gather | solution.py:102
  71.9 2.5 copy-start.2
  321.6 3.1 copy-start.1
Sparse Core Ops, SparseCore 0:
  10.0 61.9 all-gather.1
where the time goes:
time: 629 us; the launch traced here: 617 us
  blocking collectives  373 us (59%)
  matrix products  70.7 us (11%)
  local copies, waits for them, and re-layouts  69.3 us (11%)
  waiting for transfers between devices  53.8 us (9%)
  other arithmetic  36.1 us (6%)
  between operations  13.9 us (2%)
    all_to_all x1, blocking collectives, per_device(): lax.all_to_all(outgoing, ('ctx', 'tensor'), split_axis=0, concat_axis=2,...  189 us
    all_to_all x1, blocking collectives, per_device(): lax.all_to_all(partial_value.reshape(item_count, n_ctx * n_tensor, quarte...  184 us
    all_gather x1, waiting for transfers between devices, per_device(): shard_piece = lax.all_gather(stacked, 'ctx', axis=1, tiled=True)  53.7 us
    convert_element_type x2, local copies, waits for them, and re-layouts, expert_block(): widened = full_rows.astype(jnp.float32)  31.7 us
    dot_general x1, matrix products, attend_block(): jnp.einsum('kgqt,tkd->kgqd', weights.astype(jnp.bfloat16), value_block, p...  26 us
    convert_element_type x2, local copies, waits for them, and re-layouts, per_device(): partial_value.reshape(item_count, n_ctx * n_tensor, quarter)  19 us
    dot_general x1, matrix products, attend_block(): jnp.einsum('qkgd,tkd->kgqt', query_heads, key_block, preferred_element_ty...  14.3 us
    dot_general x1, matrix products, expert_block(): return jnp.dot(activated, w_down, preferred_element_type=jnp.float32)  14.3 us
  transfers between devices with their start and end apart: 1, of which 1 were waited for; matrix products, arithmetic and copies ran while one was open for 2% of the time, Pallas kernels for 0%

commit v1 on v0

v1 whole, which is shorter than its diff:
```python
import math

import jax
import jax.numpy as jnp
from jax import lax
from jax.experimental import pallas as pl
from jax.experimental.pallas import tpu as pltpu
from jax.sharding import Mesh, PartitionSpec as P

HEADS = 24
KV_HEADS = 4
HEAD_DIM = 128
EXPERTS = 8
TOP = 2
CAP = 36
EPS = 1e-05
NEG = -1e30
VMEM_LIMIT = 60 * 1024 * 1024

bf16 = jnp.bfloat16
f32 = jnp.float32


def pick_table(ids_ref):
    n = ids_ref.shape[1]
    first, second = ids_ref[0:1, :], ids_ref[1:2, :]
    expert = lax.broadcasted_iota(jnp.int32, (EXPERTS, n), 0)
    member = ((first == expert) | (second == expert)).astype(bf16)
    earlier = (
        lax.broadcasted_iota(jnp.int32, (n, n), 0) < lax.broadcasted_iota(jnp.int32, (n, n), 1)
    ).astype(bf16)
    rank = jnp.dot(member, earlier, preferred_element_type=f32).astype(jnp.int32)
    slot = lax.broadcasted_iota(jnp.int32, (EXPERTS * CAP, n), 0)
    place = jnp.full((EXPERTS * CAP, n), -1, jnp.int32)
    for e in range(EXPERTS):
        inside = (slot >= e * CAP) & (slot < (e + 1) * CAP)
        named = (first == e) | (second == e)
        place = jnp.where(inside & named, e * CAP + rank[e : e + 1, :], place)
    return place == slot, slot


def attend_kernel(where_ref, ids_ref, q_ref, res_ref, kv_ref, hid_ref, buf_ref, k_all, v_all, own, sems):
    n_w = kv_ref.shape[0]
    n_z = kv_ref.shape[1] - 1
    rows = q_ref.shape[0]
    mine, z = where_ref[0], where_ref[1]
    copies = []
    for w in range(n_w):
        src = lax.rem(mine + w, n_w)
        for s in range(n_z):
            if s == 0:
                slot = n_z if w == 0 else jnp.where(src < mine, n_z, z)
            else:
                slot = lax.rem(z + s, n_z)
            at = (w * n_z + s) * rows
            copies.append(
                pltpu.make_async_copy(kv_ref.at[src, slot, 0], k_all.at[pl.ds(at, rows)], sems.at[w])
            )
            copies.append(
                pltpu.make_async_copy(kv_ref.at[src, slot, 1], v_all.at[pl.ds(at, rows)], sems.at[w])
            )
    own_copy = pltpu.make_async_copy(kv_ref.at[mine, z], own, sems.at[n_w])
    for c in copies:
        c.start()
    own_copy.start()
    pick, _ = pick_table(ids_ref)
    for c in copies:
        c.wait()
    own_copy.wait()

    scale = math.log2(math.e) / math.sqrt(HEAD_DIM)
    group = q_ref.shape[1] // HEAD_DIM
    step = 1024
    row_at = lax.broadcasted_iota(jnp.int32, (rows, rows), 0)
    col_at = lax.broadcasted_iota(jnp.int32, (rows, rows), 1)
    tract = col_at <= row_at
    tdot = (((1,), (1,)), ((), ()))
    for h in range(group):
        cols = slice(h * HEAD_DIM, (h + 1) * HEAD_DIM)
        q = q_ref[:, cols]
        s_tract = lax.dot_general(q, k_all[0:rows], tdot, preferred_element_type=f32)
        s_cache = lax.dot_general(q, own[0], tdot, preferred_element_type=f32)
        s_own = jnp.where(tract, s_tract, s_cache) * scale
        m = jnp.max(s_own, axis=1, keepdims=True)
        p = jnp.exp2(s_own - m)
        l = jnp.sum(p, axis=1, keepdims=True)
        low = p.astype(bf16)
        zero = jnp.zeros_like(low)
        acc = jnp.dot(jnp.where(tract, low, zero), v_all[0:rows], preferred_element_type=f32)
        acc += jnp.dot(jnp.where(tract, zero, low), own[1], preferred_element_type=f32)
        for j in range(0, k_all.shape[0], step):
            lo = max(j, rows)
            k = k_all[lo : j + step]
            s = lax.dot_general(q, k, tdot, preferred_element_type=f32) * scale
            m_new = jnp.maximum(m, jnp.max(s, axis=1, keepdims=True))
            fade = jnp.exp2(m - m_new)
            p = jnp.exp2(s - m_new)
            l = l * fade + jnp.sum(p, axis=1, keepdims=True)
            acc = acc * fade + jnp.dot(p.astype(bf16), v_all[lo : j + step], preferred_element_type=f32)
            m = m_new
        hid_ref[:, cols] = (res_ref[:, cols].astype(f32) + acc / l).astype(bf16)
    buf_ref[...] = jnp.dot(pick.astype(bf16), hid_ref[...], preferred_element_type=f32).astype(bf16)


def attend(where, ids, queries, residual, kv):
    rows, width = queries.shape
    n_w, n_z = kv.shape[0], kv.shape[1] - 1
    keys = n_w * n_z * rows
    vm = pl.BlockSpec(memory_space=pltpu.VMEM)
    return pl.pallas_call(
        attend_kernel,
        out_shape=(
            jax.ShapeDtypeStruct((rows, width), bf16),
            jax.ShapeDtypeStruct((EXPERTS * CAP, width), bf16),
        ),
        in_specs=[pl.BlockSpec(memory_space=pltpu.SMEM), vm, vm, vm, pl.BlockSpec(memory_space=pl.ANY)],
        out_specs=(vm, vm),
        scratch_shapes=[
            pltpu.VMEM((keys, HEAD_DIM), bf16),
            pltpu.VMEM((keys, HEAD_DIM), bf16),
            pltpu.VMEM((2, rows, HEAD_DIM), bf16),
            pltpu.SemaphoreType.DMA((n_w + 1,)),
        ],
        compiler_params=pltpu.CompilerParams(vmem_limit_bytes=VMEM_LIMIT),
        name="attend",
    )(where, ids, queries, residual, kv)


def expert_kernel(
    x_ref, gain_ref, wg0, wu0, wd0, wg1, wu1, wd1, out_ref, x_v, g_v, u_v, d_v, normed, act, res, x_sem, w_sem, o_sem
):
    n_y, n_x, rows, width = x_ref.shape
    x_copies = [
        [pltpu.make_async_copy(x_ref.at[y, i], x_v.at[y, i], x_sem.at[y, i]) for i in range(n_x)]
        for y in range(n_y)
    ]
    w_copies = []
    for part, (g, u, d) in enumerate(((wg0, wu0, wd0), (wg1, wu1, wd1))):
        w_copies.append(
            (
                pltpu.make_async_copy(g, g_v.at[part], w_sem.at[part, 0]),
                pltpu.make_async_copy(u, u_v.at[part], w_sem.at[part, 1]),
                pltpu.make_async_copy(d, d_v.at[part], w_sem.at[part, 2]),
            )
        )
    for c in x_copies[0]:
        c.start()
    w_copies[0][0].start()
    w_copies[0][1].start()
    for c in x_copies[1]:
        c.start()
    w_copies[1][0].start()
    w_copies[1][1].start()
    w_copies[0][2].start()
    w_copies[1][2].start()
    total = n_x * width
    ff = g_v.shape[2]
    for y in range(n_y):
        for c in x_copies[y]:
            c.wait()
        sq = jnp.zeros((rows, 1), f32)
        for i in range(n_x):
            v = x_v[y, i].astype(f32)
            sq = sq + jnp.sum(v * v, axis=1, keepdims=True)
        inverse = lax.rsqrt(sq * (1.0 / total) + EPS)
        for i in range(n_x):
            gain = gain_ref[:, i * width : (i + 1) * width]
            normed[y, :, i * width : (i + 1) * width] = (
                x_v[y, i].astype(f32) * inverse * gain
            ).astype(bf16)
        for part in range(2):
            if y == 0:
                w_copies[part][0].wait()
                w_copies[part][1].wait()
            gate = jnp.dot(normed[y], g_v[part], preferred_element_type=f32)
            up = jnp.dot(normed[y], u_v[part], preferred_element_type=f32)
            act[y, :, part * ff : (part + 1) * ff] = (gate / (1.0 + jnp.exp(-gate)) * up).astype(bf16)
    w_copies[0][2].wait()
    w_copies[1][2].wait()
    outs = []
    for y in range(n_y):
        for i in range(n_x):
            cols = slice(i * width, (i + 1) * width)
            part = jnp.dot(act[y, :, :ff], d_v[0, :, cols], preferred_element_type=f32)
            part += jnp.dot(act[y, :, ff:], d_v[1, :, cols], preferred_element_type=f32)
            res[y, i] = part.astype(bf16)
            outs.append(pltpu.make_async_copy(res.at[y, i], out_ref.at[y, i], o_sem.at[y, i]))
            outs[-1].start()
    for c in outs:
        c.wait()


def experts(x, gain, own, other):
    n_y, n_x, rows, width = x.shape
    total, ff = own[0].shape
    hbm = pl.BlockSpec(memory_space=pl.ANY)
    vm = pl.BlockSpec(memory_space=pltpu.VMEM)
    return pl.pallas_call(
        expert_kernel,
        out_shape=jax.ShapeDtypeStruct(x.shape, bf16),
        in_specs=[hbm, vm] + [hbm] * 6,
        out_specs=hbm,
        scratch_shapes=[
            pltpu.VMEM(x.shape, bf16),
            pltpu.VMEM((2, total, ff), bf16),
            pltpu.VMEM((2, total, ff), bf16),
            pltpu.VMEM((2, ff, total), bf16),
            pltpu.VMEM((n_y, rows, total), bf16),
            pltpu.VMEM((n_y, rows, 2 * ff), bf16),
            pltpu.VMEM(x.shape, bf16),
            pltpu.SemaphoreType.DMA((n_y, n_x)),
            pltpu.SemaphoreType.DMA((2, 3)),
            pltpu.SemaphoreType.DMA((n_y, n_x)),
        ],
        compiler_params=pltpu.CompilerParams(vmem_limit_bytes=VMEM_LIMIT),
        name="experts",
    )(x, gain, *own, *other)


def mix_kernel(ids_ref, gates_ref, hid_ref, parts_ref, out_ref):
    pick, slot = pick_table(ids_ref)
    n = ids_ref.shape[1]
    weight = jnp.zeros((EXPERTS * CAP, n), f32)
    for e in range(EXPERTS):
        inside = (slot >= e * CAP) & (slot < (e + 1) * CAP)
        gate = jnp.where(ids_ref[0:1, :] == e, gates_ref[0:1, :], 0.0)
        gate = gate + jnp.where(ids_ref[1:2, :] == e, gates_ref[1:2, :], 0.0)
        weight = jnp.where(inside & pick, gate, weight)
    mixture = lax.dot_general(
        weight,
        parts_ref[...].astype(f32),
        (((0,), (0,)), ((), ())),
        precision=lax.Precision.HIGHEST,
        preferred_element_type=f32,
    )
    out_ref[...] = (hid_ref[...].astype(f32) + mixture).astype(bf16)


def mix(ids, gates, hidden, parts):
    vm = pl.BlockSpec(memory_space=pltpu.VMEM)
    return pl.pallas_call(
        mix_kernel,
        out_shape=jax.ShapeDtypeStruct(hidden.shape, bf16),
        in_specs=[vm] * 4,
        out_specs=vm,
        compiler_params=pltpu.CompilerParams(vmem_limit_bytes=VMEM_LIMIT),
        name="mix",
    )(ids, gates, hidden, parts)


def per_device(
    queries, keys, values, cache_keys, cache_values, residual, norm_gain, w_gate, w_up, w_down, expert_ids, gate_weights
):
    rows, width = queries.shape
    z = lax.axis_index("zh")
    n_z = lax.axis_size("zh")
    mine = lax.axis_index(("yh", "yl", "core"))
    ids, gates = expert_ids.T, gate_weights.T

    swap = [(0, 1), (1, 0)]
    own = (w_gate, w_up, w_down)
    other = tuple(lax.ppermute(w, "core", swap) for w in own)

    tract = jnp.stack((keys, values))
    cache = jnp.stack((cache_keys, cache_values))
    above = (jnp.arange(n_z) > z)[:, None, None, None]
    sent = jnp.where(above, tract[None], cache[None])
    from_z = lax.all_to_all(sent, "zh", split_axis=0, concat_axis=0, tiled=True)
    payload = jnp.concatenate((from_z, tract[None]))
    kv = lax.all_gather(payload, ("yh", "yl", "core"), axis=0, tiled=False)

    where = jnp.stack((mine, z)).astype(jnp.int32)
    hidden, buffer = attend(where, ids, queries, residual, kv)

    arrived = lax.all_to_all(
        buffer.reshape(EXPERTS, CAP, width), ("zh", "yh"), split_axis=0, concat_axis=0, tiled=True
    ).reshape(EXPERTS * CAP, width)
    gathered = lax.all_gather(arrived, ("yl", "x"), axis=0, tiled=False)
    n_x = lax.axis_size("x")
    partial = experts(
        gathered.reshape(-1, n_x, EXPERTS * CAP, width), norm_gain.reshape(1, -1), own, other
    )
    summed = lax.psum_scatter(
        partial.reshape(-1, width), ("yl", "x"), scatter_dimension=0, tiled=True
    )
    back = lax.all_to_all(
        summed.reshape(EXPERTS, CAP, width), ("zh", "yh"), split_axis=0, concat_axis=0, tiled=True
    ).reshape(EXPERTS * CAP, width)
    return mix(ids, gates, hidden, back)


def solution(mesh):
    fine = Mesh(mesh.devices.reshape(2, 4, 2, 2, 2, 4), ("dp", "zh", "yh", "yl", "core", "x"))
    ctx = ("zh", "yh", "yl", "core")
    tok = P(("dp",) + ctx, "x")
    in_specs = (
        tok, tok, tok, tok, tok, tok,
        P(),
        P(None, ctx + ("x",)),
        P(None, ctx + ("x",)),
        P(ctx + ("x",), None),
        P(("dp",) + ctx, None),
        P(("dp",) + ctx, None),
    )
    return jax.shard_map(per_device, mesh=fine, in_specs=in_specs, out_specs=tok, check_vma=False)
```

time: 629 us -> 244 us (0.39); the launches traced: 617 us -> 243 us
  blocking collectives: 373 us -> 64.1 us
  matrix products: 70.7 us -> 0 us
  waiting for transfers between devices: 53.8 us -> 120 us
  local copies, waits for them, and re-layouts: 69.3 us -> 9.2 us
  Pallas kernels: 0 us -> 33.8 us
  other arithmetic: 36.1 us -> 2.33 us
    all_to_all x2 -> x3, blocking collectives: 373 us -> 64.1 us  [the longest x1 23.2 us: per_device(): lax.all_to_all(buffer.reshape(EXPERTS, CAP, width), ('zh', 'yh'), split_a...]
    dot_general x6 -> x0, matrix products: 70.7 us -> none  [the longest x1 26 us: attend_block(): jnp.einsum('kgqt,tkd->kgqd', weights.astype(jnp.bfloat16), value_block, p...]
    convert_element_type x4 -> x0, local copies, waits for them, and re-layouts: 50.6 us -> none  [the longest x2 31.7 us: expert_block(): widened = full_rows.astype(jnp.float32)]
    reduce_scatter x0 -> x1, waiting for transfers between devices: none -> 50.2 us  [per_device(): lax.psum_scatter(partial.reshape(-1, width), ('yl', 'x'), scatter_dimensi...]
    pallas_call x0 -> x3, Pallas kernels: none -> 33.8 us  [the longest x1 17.1 us: experts(): pl.pallas_call(expert_kernel, out_shape=jax.ShapeDtypeStruct(x.shape, bf1...]
    reduce_sum x6 -> x0, other arithmetic: 18.6 us -> none  [the longest x1 11.4 us: attend_block(): run_sum = jnp.sum(weights, axis=-1)]
    ppermute x0 -> x3, waiting for transfers between devices: none -> 12.2 us  [per_device(): other = tuple((lax.ppermute(w, 'core', swap) for w in own))]
    convert_element_type x2 -> x0, other arithmetic: 9.99 us -> none  [the longest x1 9.99 us: expert_block(): widened = full_rows.astype(jnp.float32)]
  transfers between devices with their start and end apart: 1 -> 6, of which waited for: 1 -> 5; matrix products, arithmetic and copies ran while one was open for 2% -> 0% of each run, Pallas kernels for 0% -> 0%
where the time goes in v1:
time: 244 us; the launch traced here: 243 us
  waiting for transfers between devices  120 us (49%)
  blocking collectives  64.1 us (26%)
  Pallas kernels  33.8 us (14%)
  between operations  13.2 us (5%)
  local copies, waits for them, and re-layouts  9.2 us (4%)
    reduce_scatter x1, waiting for transfers between devices, per_device(): lax.psum_scatter(partial.reshape(-1, width), ('yl', 'x'), scatter_dimensi...  50.2 us
    all_gather x1, waiting for transfers between devices, per_device(): gathered = lax.all_gather(arrived, ('yl', 'x'), axis=0, tiled=False)  31.6 us
    all_gather x1, waiting for transfers between devices, per_device(): kv = lax.all_gather(payload, ('yh', 'yl', 'core'), axis=0, tiled=False)  25.9 us
    all_to_all x1, blocking collectives, per_device(): lax.all_to_all(buffer.reshape(EXPERTS, CAP, width), ('zh', 'yh'), split_a...  23.2 us
    all_to_all x1, blocking collectives, per_device(): lax.all_to_all(summed.reshape(EXPERTS, CAP, width), ('zh', 'yh'), split_a...  22.6 us
    all_to_all x1, blocking collectives, per_device(): from_z = lax.all_to_all(sent, 'zh', split_axis=0, concat_axis=0, tiled=True)  18.4 us
    pallas_call x1, Pallas kernels, experts(): pl.pallas_call(expert_kernel, out_shape=jax.ShapeDtypeStruct(x.shape, bf1...  17.1 us
    pallas_call x1, Pallas kernels, attend(): pl.pallas_call(attend_kernel, out_shape=(jax.ShapeDtypeStruct((rows, widt...  13.9 us
  transfers between devices with their start and end apart: 6, of which 5 were waited for; matrix products, arithmetic and copies ran while one was open for 0% of the time, Pallas kernels for 0%

profile of v1, /device:TPU:32, one launch (start us, length us, event | category | flops | bytes accessed | tf_op | source)
XLA Modules:
  0.0 243.3 jit_solution(12684530843898649112)
XLA Ops:
  6.5 0.0 all-gather.6.cloned.1.call-start
  6.5 0.8 pad_maximum_fusion.1
  7.4 0.1 broadcast_select_fusion
  7.5 18.4 %all_to_all.15 = bf16[4,2,128,128]{3,2,1,0:T(8,128)(2,1)S(1)} all-to-all(bf16[4,2,128,128]{3,2,1,0:T(8,128)(2,1)S(1)} %broadcast_select_fusion), channel_id=1, replica_groups=mesh['dp'=2,'zh'=4,'yh'=2,'yl'=2,'core'=2,'x'=4] {'zh'}, dimensions={0} | all-to-all | bytes 524288 | tf_op jit(solution)/shard_map/all_to_all | solution.py:268
  25.8 0.8 pad_maximum_fusion
  26.6 0.0 all-gather.6.cloned.1.call-update
  26.6 0.0 all-gather.4.cloned.1.call-start
  26.7 0.6 pad_add_fusion.where_ref
  27.3 25.9 %all-gather.6.cloned.1.call-done = bf16[40,2,128,128]{3,2,1,0:T(8,128)(2,1)} async-done(((bf16[5,2,128,128]{3,2,1,0:T(8,128)(2,1)}), bf16[40,2,128,128]{3,2,1,0:T(8,128)(2,1)}) %all-gather.6.cloned.1.call-update) | async-done | bytes 2621456 | tf_op jit(solution)/shard_map/all_gather | solution.py:270
  53.2 0.0 copy-start
  53.2 13.9 %attend.1 = (bf16[128,768]{1,0:T(8,128)(2,1)}, bf16[288,768]{1,0:T(8,128)(2,1)}) custom-call(s32[2]{0:T(128)} %pad_add_fusion.where_ref, s32[2,128]{1,0:T(2,128)} %bitcast.22, bf16[128,768]{1,0:T(8,128)(2,1)} %q_ref.1, bf16[128,768]{1,0:T(8,128)(2,1)} %res_ref.1, bf16[8,5,2,128,128]{4,3,2,1,0:T(8,128)(2,1)} %bitcast.16), custom_call_target="tpu_custom_call" | custom-call | tf_op jit(solution)/shard_map/attend/pallas_call | solution.py:110
  67.1 1.9 reshape.24
  69.0 23.2 %all_to_all.16 = bf16[8,36,768]{2,1,0:T(8,128)(2,1)} all-to-all(bf16[8,36,768]{2,1,0:T(8,128)(2,1)} %reshape.24), channel_id=1, replica_groups=mesh['dp'=2,'zh'=4,'yh'=2,'yl'=2,'core'=2,'x'=4] {'zh','yh'}, dimensions={0} | all-to-all | bytes 884736 | tf_op jit(solution)/shard_map/all_to_all | solution.py:275
  92.2 1.9 all_gather_reshape.3
  94.1 0.0 all-gather.4.cloned.1.call-update
  94.1 0.0 reduce-scatter.2.cloned.1.call-start
  94.2 0.0 copy-done
  94.2 0.1 collective-permute-start
  94.3 0.5 collective-permute-start.1
  94.8 0.1 collective-permute-start.2
  94.9 8.5 %collective-permute-done.wg1 = bf16[3072,512]{1,0:T(8,128)(2,1)S(1)} collective-permute-done((bf16[3072,512]{1,0:T(8,128)(2,1)S(1)}, bf16[3072,512]{1,0:T(8,128)(2,1)S(1)}, u32[]{:S(2)}, u32[]{:S(2)}) %collective-permute-start) | collective-permute-done | bytes 3145760 | tf_op jit(solution)/shard_map/ppermute | solution.py:262
  103.4 0.0 copy-start.1
  103.4 1.7 copy-done.1
  105.1 3.6 %collective-permute-done.1.wu1 = bf16[3072,512]{1,0:T(8,128)(2,1)S(1)} collective-permute-done((bf16[3072,512]{1,0:T(8,128)(2,1)}, bf16[3072,512]{1,0:T(8,128)(2,1)S(1)}, u32[]{:S(2)}, u32[]{:S(2)}) %collective-permute-start.1) | collective-permute-done | bytes 3145760 | tf_op jit(solution)/shard_map/ppermute | solution.py:262
  108.8 0.0 copy-start.2
  108.8 1.7 copy-done.2
  110.5 0.0 collective-permute-done.2.wd1
  110.5 31.6 %all-gather.4.cloned.1.call-done = bf16[8,288,768]{2,1,0:T(8,128)(2,1)} async-done(((bf16[1,288,768]{2,1,0:T(8,128)(2,1)}), bf16[8,288,768]{2,1,0:T(8,128)(2,1)}) %all-gather.4.cloned.1.call-update) | async-done | bytes 3538960 | tf_op jit(solution)/shard_map/all_gather | solution.py:278
  142.1 17.1 %experts.1 = bf16[2,4,288,768]{3,2,1,0:T(8,128)(2,1)} custom-call(bf16[2,4,288,768]{3,2,1,0:T(8,128)(2,1)} %bitcast.15, f32[1,3072]{1,0:T(1,128)} %bitcast.21, bf16[3072,512]{1,0:T(8,128)(2,1)} %wg0.1, bf16[3072,512]{1,0:T(8,128)(2,1)} %wu0.1, bf16[512,3072]{1,0:T(8,128)(2,1)} %wd0.1, bf16[3072,512]{1,0:T(8,128)(2,1)} %copy-done.1, ...), custom_call_target="tpu_custom_call" | custom-call | tf_op jit(solution)/shard_map/experts/pallas_call | solution.py:198
  159.3 0.0 reduce-scatter.2.cloned.1.call-update
  159.3 50.2 %reduce-scatter.2.cloned.1.call-done = bf16[288,768]{1,0:T(8,128)(2,1)} async-done(((bf16[2304,768]{1,0:T(8,128)(2,1)}), bf16[288,768]{1,0:T(8,128)(2,1)}) %reduce-scatter.2.cloned.1.call-update) | async-done | bytes 442384 | tf_op jit(solution)/shard_map/reduce_scatter | solution.py:283
  209.5 1.1 reshape.28
  210.6 22.6 %all_to_all.17 = bf16[8,36,768]{2,1,0:T(8,128)(2,1)S(1)} all-to-all(bf16[8,36,768]{2,1,0:T(8,128)(2,1)S(1)} %reshape.28), channel_id=1, replica_groups=mesh['dp'=2,'zh'=4,'yh'=2,'yl'=2,'core'=2,'x'=4] {'zh','yh'}, dimensions={0} | all-to-all | bytes 884736 | tf_op jit(solution)/shard_map/all_to_all | solution.py:286
  233.1 0.9 reshape.29.parts_ref
  234.0 2.8 %mix.1 = bf16[128,768]{1,0:T(8,128)(2,1)} custom-call(s32[2,128]{1,0:T(2,128)} %bitcast.23, f32[2,128]{1,0:T(2,128)} %bitcast.24, bf16[128,768]{1,0:T(8,128)(2,1)} %get-tuple-element.7.hid_ref, bf16[288,768]{1,0:T(8,128)(2,1)} %reshape.29.parts_ref), custom_call_target="tpu_custom_call" | custom-call | tf_op jit(solution)/shard_map/mix/pallas_call | solution.py:241
  (1 shorter events, 0.0 us)
Async XLA Ops:
  6.5 46.7 %all-gather.6.cloned.1.call-start = ((), (), s32[]{:S(2)}) async-start(), calls=%async_computation.6 | async-start | bytes 2949120 | tf_op jit(solution)/shard_map/all_gather | solution.py:270
  26.6 115.5 %all-gather.4.cloned.1.call-start = ((), (), s32[]{:S(2)}) async-start(), calls=%async_computation.4 | async-start | bytes 3981312 | tf_op jit(solution)/shard_map/all_gather | solution.py:278
  53.2 40.9 %copy-start = (bf16[3072,512]{1,0:T(8,128)(2,1)S(1)}, bf16[3072,512]{1,0:T(8,128)(2,1)}, u32[]{:S(2)}) copy-start(bf16[3072,512]{1,0:T(8,128)(2,1)} %wg0.1) | copy-start | bytes 9437188
  94.1 115.3 %reduce-scatter.2.cloned.1.call-start = ((), (), s32[]{:S(2)}) async-start(), calls=%async_computation.5 | async-start | bytes 3981312 | tf_op jit(solution)/shard_map/reduce_scatter | solution.py:283
  94.2 9.2 %collective-permute-start = (bf16[3072,512]{1,0:T(8,128)(2,1)S(1)}, bf16[3072,512]{1,0:T(8,128)(2,1)S(1)}, u32[]{:S(2)}, u32[]{:S(2)}) collective-permute-start(bf16[3072,512]{1,0:T(8,128)(2,1)S(1)} %copy-done), channel_id=1, source_target_pairs={{0,4},{4,0},{1,5},{5,1},{2,6},{6,2},{3,7},{7,3},{8,12},{12,8},{9,1... | collective-permute-start | bytes 9437192 | tf_op jit(solution)/shard_map/ppermute | solution.py:262
  94.3 14.5 %collective-permute-start.1 = (bf16[3072,512]{1,0:T(8,128)(2,1)}, bf16[3072,512]{1,0:T(8,128)(2,1)S(1)}, u32[]{:S(2)}, u32[]{:S(2)}) collective-permute-start(bf16[3072,512]{1,0:T(8,128)(2,1)} %wu0.1), channel_id=1, source_target_pairs={{0,4},{4,0},{1,5},{5,1},{2,6},{6,2},{3,7},{7,3},{8,12},{12,8},{9,1... | collective-permute-start | bytes 9437192 | tf_op jit(solution)/shard_map/ppermute | solution.py:262
  94.8 15.7 %collective-permute-start.2 = (bf16[512,3072]{1,0:T(8,128)(2,1)}, bf16[512,3072]{1,0:T(8,128)(2,1)}, u32[]{:S(2)}, u32[]{:S(2)}) collective-permute-start(bf16[512,3072]{1,0:T(8,128)(2,1)} %wd0.1), channel_id=1, source_target_pairs={{0,4},{4,0},{1,5},{5,1},{2,6},{6,2},{3,7},{7,3},{8,12},{12,8},{9,1... | collective-permute-start | bytes 9437192 | tf_op jit(solution)/shard_map/ppermute | solution.py:262
  103.4 1.7 copy-start.1
  108.8 1.7 copy-start.2
Sparse Core Ops, SparseCore 0:
  26.8 26.4 all-gather.5
  94.2 47.8 all-gather.3
  159.4 50.0 reduce-scatter.1

commit v2 on v0

v2 whole, which is shorter than its diff:
```python
import math

import jax
import jax.numpy as jnp
from jax import lax
from jax.experimental import pallas as pl
from jax.experimental.pallas import tpu as pltpu
from jax.sharding import Mesh, PartitionSpec as P

HEADS = 24
KV_HEADS = 4
HEAD_DIM = 128
EXPERTS = 8
TOP = 2
CAP = 36
PAD = 40
EPS = 1e-05
NZ, NY, NX, NC = 4, 4, 4, 2
SHIFTS = (1, 3, 2)
MB = 1024 * 1024

bf16 = jnp.bfloat16
f32 = jnp.float32
VM = pl.BlockSpec(memory_space=pltpu.VMEM)
SM = pl.BlockSpec(memory_space=pltpu.SMEM)
HBM = pl.BlockSpec(memory_space=pltpu.HBM)


def call(body, out_shape, args, name, scratch=(), limit=16, scalars=0, hbm=0):
    many = isinstance(out_shape, list)
    return pl.pallas_call(
        body,
        out_shape=out_shape,
        in_specs=[SM] * scalars + [VM] * (len(args) - scalars - hbm) + [HBM] * hbm,
        out_specs=[VM] * len(out_shape) if many else VM,
        scratch_shapes=list(scratch),
        compiler_params=pltpu.CompilerParams(vmem_limit_bytes=limit * MB),
        name=name,
    )(*args)


def pick_table(ids_ref):
    n = ids_ref.shape[1]
    first, second = ids_ref[0:1, :], ids_ref[1:2, :]
    line = lax.broadcasted_iota(jnp.int32, (EXPERTS, n), 0)
    named = (first == line) | (second == line)
    earlier = (
        lax.broadcasted_iota(jnp.int32, (n, n), 0) < lax.broadcasted_iota(jnp.int32, (n, n), 1)
    ).astype(bf16)
    rank = jnp.dot(named.astype(bf16), earlier, preferred_element_type=f32).astype(jnp.int32)
    rank = jnp.where(named, rank, -1)
    row = lax.broadcasted_iota(jnp.int32, (PAD, n), 0)
    return [rank[e : e + 1, :] == row for e in range(EXPERTS)]


def attend_kernel(where_ref, ids_ref, *refs):
    kv_refs = refs[: NY * NC]
    q_hbm, res_hbm, hid_ref, buf_ref, q_all, o_all, q_ref, res_ref, sems = refs[NY * NC :]
    q_load = pltpu.make_async_copy(q_hbm, q_ref, sems.at[0])
    res_load = pltpu.make_async_copy(res_hbm, res_ref, sems.at[1])
    q_load.start()
    res_load.start()
    rows, width = q_ref.shape
    q_load.wait()
    heads = width // HEAD_DIM
    y, core = where_ref[1], where_ref[2]
    mine = y * NC + core
    span = kv_refs[0].shape[1] - rows
    for h in range(heads):
        q_all[h * rows : (h + 1) * rows, :] = q_ref[:, h * HEAD_DIM : (h + 1) * HEAD_DIM]
    starts = [0]
    for i, shift in enumerate((0,) + SHIFTS):
        for c in range(NC):
            if i + c:
                src = lax.rem(y - shift + NY, NY) * NC + lax.rem(core + c, NC)
                starts.append(pl.multiple_of(jnp.where(src < mine, 0, rows), rows))

    scale = math.log2(math.e) / math.sqrt(HEAD_DIM)
    tile = 2 * rows
    row_at = lax.rem(lax.broadcasted_iota(jnp.int32, (tile, rows), 0), rows)
    col_at = lax.broadcasted_iota(jnp.int32, (tile, rows), 1)
    tract = col_at <= row_at
    tdot = (((1,), (1,)), ((), ()))

    def group(g, carry):
        at = pl.ds(pl.multiple_of(g * tile, tile), tile)
        q = q_all[at, :]
        s_tract = lax.dot_general(q, kv_refs[0][0, 0:rows], tdot, preferred_element_type=f32)
        s_cache = lax.dot_general(q, kv_refs[0][0, span:], tdot, preferred_element_type=f32)
        s = jnp.where(tract, s_tract, s_cache) * scale
        m = jnp.max(s, axis=1, keepdims=True)
        p = jnp.exp2(s - m)
        l = jnp.sum(p, axis=1, keepdims=True)
        low = p.astype(bf16)
        zero = jnp.zeros_like(low)
        acc = jnp.dot(jnp.where(tract, low, zero), kv_refs[0][1, 0:rows], preferred_element_type=f32)
        acc += jnp.dot(jnp.where(tract, zero, low), kv_refs[0][1, span:], preferred_element_type=f32)
        for i, (ref, start) in enumerate(zip(kv_refs, starts)):
            keys = pl.ds(start, span) if i else pl.ds(rows, span - rows)
            s = lax.dot_general(q, ref[0, keys], tdot, preferred_element_type=f32) * scale
            m_new = jnp.maximum(m, jnp.max(s, axis=1, keepdims=True))
            fade = jnp.exp2(m - m_new)
            p = jnp.exp2(s - m_new)
            l = l * fade + jnp.sum(p, axis=1, keepdims=True)
            acc = acc * fade + jnp.dot(p.astype(bf16), ref[1, keys], preferred_element_type=f32)
            m = m_new
        o_all[at, :] = acc / l
        return carry

    lax.fori_loop(0, heads * rows // tile, group, 0)
    res_load.wait()
    for h in range(heads):
        cols = slice(h * HEAD_DIM, (h + 1) * HEAD_DIM)
        attended = o_all[h * rows : (h + 1) * rows, :]
        hid_ref[:, cols] = (res_ref[:, cols].astype(f32) + attended).astype(bf16)
    table = jnp.concatenate([t.astype(f32) for t in pick_table(ids_ref)], axis=0).astype(bf16)
    routed = jnp.dot(table, hid_ref[...], preferred_element_type=f32).astype(bf16)
    for e in range(EXPERTS):
        buf_ref[e] = routed[e * PAD : e * PAD + CAP]


def attend(where, ids, queries, residual, kv):
    rows, width = queries.shape
    heads = width // HEAD_DIM
    return call(
        attend_kernel,
        [
            jax.ShapeDtypeStruct((rows, width), bf16),
            jax.ShapeDtypeStruct((EXPERTS, CAP, width), bf16),
        ],
        [where, ids, *kv, queries, residual],
        "attend",
        [
            pltpu.VMEM((heads * rows, HEAD_DIM), bf16),
            pltpu.VMEM((heads * rows, HEAD_DIM), f32),
            pltpu.VMEM((rows, width), bf16),
            pltpu.VMEM((rows, width), bf16),
            pltpu.SemaphoreType.DMA((2,)),
        ],
        limit=16,
        scalars=1,
        hbm=2,
    )


def expert_kernel(where_ref, gain_ref, *refs):
    a_own, a_far, b_all = refs[0:NX], refs[NX : 2 * NX], refs[2 * NX : 3 * NX]
    weights = refs[3 * NX : 3 * NX + 6]
    a_out = refs[3 * NX + 6 : 5 * NX + 6]
    b_out = refs[5 * NX + 6 : 6 * NX + 6]
    normed, act, *held, sems = refs[6 * NX + 6 :]
    rows, width = a_own[0].shape
    full = 2 * width
    total, ff = weights[0].shape
    loads = [pltpu.make_async_copy(w, v, sems.at[i]) for i, (w, v) in enumerate(zip(weights, held))]
    for i in (0, 1, 3, 4, 2, 5):
        loads[i].start()
    weights = held
    x = where_ref[3]
    order = (0,) + SHIFTS
    for r in range(2):
        a = a_own if r == 0 else a_far
        at = slice(r * rows, (r + 1) * rows)
        sq = jnp.zeros((rows, 1), f32)
        for i in range(NX):
            v = a[i][...].astype(f32)
            sq = sq + jnp.sum(v * v, axis=1, keepdims=True)
            v = b_all[i][r].astype(f32)
            sq = sq + jnp.sum(v * v, axis=1, keepdims=True)
        inverse = lax.rsqrt(sq * (1.0 / total) + EPS)
        for i, shift in enumerate(order):
            src = lax.rem(x - shift + NX, NX)
            gain = gain_ref[src]
            start = pl.multiple_of(src * full, full)
            v = a[i][...].astype(f32) * inverse * gain[:, :width]
            normed[at, pl.ds(start, width)] = v.astype(bf16)
            v = b_all[i][r].astype(f32) * inverse * gain[:, width:]
            normed[at, pl.ds(start + width, width)] = v.astype(bf16)
    for part in range(2):
        w_gate, w_up, _ = weights[3 * part : 3 * part + 3]
        loads[3 * part].wait()
        loads[3 * part + 1].wait()
        gate = jnp.dot(normed[...], w_gate[...], preferred_element_type=f32)
        up = jnp.dot(normed[...], w_up[...], preferred_element_type=f32)
        act[:, part * ff : (part + 1) * ff] = (gate / (1.0 + jnp.exp(-gate)) * up).astype(bf16)
    loads[2].wait()
    loads[5].wait()
    for i, shift in enumerate(order):
        cols = pl.ds(pl.multiple_of(lax.rem(x + shift, NX) * full, full), full)
        out = jnp.dot(act[:, :ff], weights[2][:, cols], preferred_element_type=f32)
        out += jnp.dot(act[:, ff:], weights[5][:, cols], preferred_element_type=f32)
        for r in range(2):
            at = slice(r * rows, (r + 1) * rows)
            a_out[r * NX + i][...] = out[at, :width].astype(bf16)
            b_out[i][r] = out[at, width:].astype(bf16)


def experts(where, gain, a_own, a_far, b_all, own, other):
    rows, width = a_own[0].shape
    total, ff = own[0].shape
    out = call(
        expert_kernel,
        [jax.ShapeDtypeStruct((rows, width), bf16)] * (2 * NX)
        + [jax.ShapeDtypeStruct((2, rows, width), bf16)] * NX,
        [where, gain, *a_own, *a_far, *b_all, *own, *other],
        "experts",
        [pltpu.VMEM((2 * rows, total), bf16), pltpu.VMEM((2 * rows, 2 * ff), bf16)]
        + [pltpu.VMEM(w.shape, bf16) for w in (*own, *other)]
        + [pltpu.SemaphoreType.DMA((6,))],
        limit=47,
        scalars=1,
        hbm=6,
    )
    return out[:NX], out[NX : 2 * NX], out[2 * NX :]


def mix_kernel(ids_ref, gates_ref, hid_ref, part_ref, out_ref, held):
    weight = []
    for e, pick in enumerate(pick_table(ids_ref)):
        gate = jnp.where(ids_ref[0:1, :] == e, gates_ref[0:1, :], 0.0)
        gate = gate + jnp.where(ids_ref[1:2, :] == e, gates_ref[1:2, :], 0.0)
        weight.append(jnp.where(pick, gate, 0.0))
    held[...] = jnp.zeros_like(held)
    for e in range(EXPERTS):
        held[e * PAD : e * PAD + CAP, :] = part_ref[e].astype(f32)
    mixture = lax.dot_general(
        jnp.concatenate(weight, axis=0),
        held[...],
        (((0,), (0,)), ((), ())),
        precision=lax.Precision.HIGHEST,
        preferred_element_type=f32,
    )
    out_ref[...] = (hid_ref[...].astype(f32) + mixture).astype(bf16)


def mix(ids, gates, hidden, parts):
    return call(
        mix_kernel,
        jax.ShapeDtypeStruct(hidden.shape, bf16),
        [ids, gates, hidden, parts],
        "mix",
        [pltpu.VMEM((EXPERTS * PAD, hidden.shape[1]), f32)],
    )


def pack_kv_kernel(*refs):
    from_z, near, out_ref, sems = refs[: NZ - 1], refs[NZ - 1 : NZ + 3], refs[-2], refs[-1]
    n = near[0].shape[0]
    loads = []
    for i, ref in enumerate(near):
        at = out_ref.at[i % 2, pl.ds((i // 2) * NZ * n, n)]
        loads.append(pltpu.make_async_copy(ref, at, sems.at[i]))
        loads[-1].start()
    for i, ref in enumerate(from_z):
        out_ref[:, (i + 1) * n : (i + 2) * n] = ref[...]
    for c in loads:
        c.wait()


def split_kernel(in_ref, a_ref, b_ref):
    width = a_ref.shape[1]
    for e in range(EXPERTS):
        a_ref[e * CAP : (e + 1) * CAP, :] = in_ref[e, :, :width]
        b_ref[e * CAP : (e + 1) * CAP, :] = in_ref[e, :, width:]


def first_sum_kernel(*refs):
    a_own, a_got = refs[0:3], refs[3:6]
    b_own, b_got = refs[6], refs[7:10]
    a_out, b_out = refs[10:13], refs[13:15]
    for own, got, out in zip(a_own, a_got, a_out):
        out[...] = (own[...].astype(f32) + got[...].astype(f32)).astype(bf16)
    for r in range(2):
        total = b_own[r].astype(f32)
        for got in b_got:
            total = total + got[r].astype(f32)
        b_out[r][...] = total.astype(bf16)


def last_sum_kernel(*refs):
    a_in, b_in, out_ref = refs[0:5], refs[5:7], refs[7]
    width = a_in[0].shape[1]
    a, b = a_in[0][...].astype(f32), b_in[0][...].astype(f32)
    for ref in a_in[1:]:
        a = a + ref[...].astype(f32)
    b = b + b_in[1][...].astype(f32)
    a, b = a.astype(bf16), b.astype(bf16)
    for e in range(EXPERTS):
        out_ref[e, :, :width] = a[e * CAP : (e + 1) * CAP]
        out_ref[e, :, width:] = b[e * CAP : (e + 1) * CAP]


SWAP = [(0, 1), (1, 0)]


def turn(v, axis, shift):
    n = 4
    return lax.ppermute(v, axis, [(i, (i + shift) % n) for i in range(n)])


def swap_y(v):
    return lax.ppermute(v, "yl", SWAP)


def swap_core(v):
    return lax.ppermute(v, "core", SWAP)


def gather_kv(z, keys, values, cache_keys, cache_values):
    tract = jnp.stack((keys, values))
    cache = jnp.stack((cache_keys, cache_values))
    sent = [jnp.where(z + s < NZ, tract, cache) for s in SHIFTS]
    from_z = lax.optimization_barrier([turn(v, "zh", s) for v, s in zip(sent, SHIFTS)])
    n = keys.shape[0]
    payload = call(
        pack_kv_kernel,
        jax.ShapeDtypeStruct((2, (NZ + 1) * n, HEAD_DIM), bf16),
        [*from_z, keys, values, cache_keys, cache_values],
        "pack_kv",
        [pltpu.SemaphoreType.DMA((4,))],
        hbm=4,
    )
    got = lax.optimization_barrier(
        [turn(payload, ("yh", "yl"), s) for s in SHIFTS] + [swap_core(payload)]
    )
    far = lax.optimization_barrier([swap_core(g) for g in got[:3]])
    return [payload, got[3], got[0], far[0], got[1], far[1], got[2], far[2]]


def per_device(
    queries, keys, values, cache_keys, cache_values, residual, norm_gain, w_gate, w_up, w_down, expert_ids, gate_weights
):
    rows, width = queries.shape
    half = width // 2
    z = lax.axis_index("zh")
    y = lax.axis_index(("yh", "yl"))
    where = jnp.stack((z, y, lax.axis_index("core"), lax.axis_index("x"))).astype(jnp.int32)
    ids, gates = expert_ids.T, gate_weights.T

    own = (w_gate, w_up, w_down)
    kv = gather_kv(z, keys, values, cache_keys, cache_values)
    held = lax.optimization_barrier((own, kv[-1]))[0]
    other = tuple(swap_core(w) for w in held)

    hidden, buffer = attend(where, ids, queries, residual, kv)
    buffer, other = lax.optimization_barrier((buffer, other))
    arrived = lax.all_to_all(buffer, ("zh", "yh"), split_axis=0, concat_axis=0, tiled=True)
    slots = EXPERTS * CAP
    piece = jax.ShapeDtypeStruct((slots, half), bf16)
    a, b = call(split_kernel, [piece] * 2, [arrived], "split")

    *a_turned, a_far, b_far = lax.optimization_barrier(
        [turn(a, "x", s) for s in SHIFTS] + [swap_y(a), swap_y(b)]
    )
    b_pair = jnp.stack((b, b_far))
    moved = lax.optimization_barrier(
        [turn(b_pair, "x", s) for s in SHIFTS] + [swap_y(v) for v in a_turned]
    )
    a_own, a_far = [a] + a_turned, [a_far] + moved[3:]
    b_all = [b_pair] + moved[:3]

    gain = norm_gain.reshape(NX, 1, width)
    a_own, a_far, b_all = experts(where, gain, a_own, a_far, b_all, own, other)
    moved = lax.optimization_barrier(
        [turn(v, "x", s) for v, s in zip(b_all[1:], SHIFTS)] + [swap_y(v) for v in a_far[1:]]
    )
    *a_sums, b_own, b_far = call(
        first_sum_kernel,
        [piece] * 5,
        [*a_own[1:], *moved[3:], b_all[0], *moved[:3]],
        "first_sum",
    )
    moved = lax.optimization_barrier(
        [turn(v, "x", s) for v, s in zip(a_sums, SHIFTS)] + [swap_y(a_far[0]), swap_y(b_far)]
    )
    result = call(
        last_sum_kernel,
        jax.ShapeDtypeStruct((EXPERTS, CAP, width), bf16),
        [a_own[0], *moved[:4], b_own, moved[4]],
        "last_sum",
    )
    back = lax.all_to_all(result, ("zh", "yh"), split_axis=0, concat_axis=0, tiled=True)
    return mix(ids, gates, hidden, back)


def solution(mesh):
    fine = Mesh(mesh.devices.reshape(2, 4, 2, 2, 2, 4), ("dp", "zh", "yh", "yl", "core", "x"))
    ctx = ("zh", "yh", "yl", "core")
    tok = P(("dp",) + ctx, "x")
    in_specs = (
        tok, tok, tok, tok, tok, tok,
        P(),
        P(None, ctx + ("x",)),
        P(None, ctx + ("x",)),
        P(ctx + ("x",), None),
        P(("dp",) + ctx, None),
        P(("dp",) + ctx, None),
    )
    return jax.shard_map(per_device, mesh=fine, in_specs=in_specs, out_specs=tok, check_vma=False)
```

time: 629 us -> 193 us (0.31); the launches traced: 617 us -> 192 us
  blocking collectives: 373 us -> 43.1 us
  matrix products: 70.7 us -> 0 us
  local copies, waits for them, and re-layouts: 69.3 us -> 5.58 us
  starting transfers between devices: 0.01 us -> 43.9 us
  other arithmetic: 36.1 us -> 0.96 us
  Pallas kernels: 0 us -> 28.7 us
  waiting for transfers between devices: 53.8 us -> 69.6 us
  between operations: 13.9 us -> 0.13 us
    all_to_all x2, blocking collectives: 373 us -> 43.1 us  [the longest x1 25.4 us: per_device(): lax.all_to_all(buffer, ('zh', 'yh'), split_axis=0, concat_axis=0, tiled=T...]
    dot_general x6 -> x0, matrix products: 70.7 us -> none  [the longest x1 26 us: attend_block(): jnp.einsum('kgqt,tkd->kgqd', weights.astype(jnp.bfloat16), value_block, p...]
    ppermute x0 -> x35, waiting for transfers between devices: none -> 69.6 us  [the longest x18 41.9 us: turn(): return lax.ppermute(v, axis, [(i, (i + shift) % n) for i in range(n)])]
    all_gather x1 -> x0, waiting for transfers between devices: 53.7 us -> none  [per_device(): shard_piece = lax.all_gather(stacked, 'ctx', axis=1, tiled=True)]
    convert_element_type x4 -> x0, local copies, waits for them, and re-layouts: 50.6 us -> none  [the longest x2 31.7 us: expert_block(): widened = full_rows.astype(jnp.float32)]
    ppermute x0 -> x35, starting transfers between devices: none -> 43.9 us  [the longest x18 32.9 us: turn(): return lax.ppermute(v, axis, [(i, (i + shift) % n) for i in range(n)])]
    pallas_call x0 -> x7, Pallas kernels: none -> 28.7 us  [call(): pl.pallas_call(body, out_shape=out_shape, in_specs=[SM] * scalars + [VM]...]
    reduce_sum x6 -> x0, other arithmetic: 18.6 us -> none  [the longest x1 11.4 us: attend_block(): run_sum = jnp.sum(weights, axis=-1)]
  transfers between devices with their start and end apart: 1 -> 35, of which waited for: 1 -> 19; matrix products, arithmetic and copies ran while one was open for 2% -> 0% of each run, Pallas kernels for 0% -> 6%
where the time goes in v2:
time: 193 us; the launch traced here: 192 us
  waiting for transfers between devices  69.6 us (36%)
  starting transfers between devices  43.9 us (23%)
  blocking collectives  43.1 us (22%)
  Pallas kernels  28.7 us (15%)
  local copies, waits for them, and re-layouts  5.58 us (3%)
    ppermute x18, waiting for transfers between devices, turn(): return lax.ppermute(v, axis, [(i, (i + shift) % n) for i in range(n)])  41.9 us
    ppermute x18, starting transfers between devices, turn(): return lax.ppermute(v, axis, [(i, (i + shift) % n) for i in range(n)])  32.9 us
    pallas_call x7, Pallas kernels, call(): pl.pallas_call(body, out_shape=out_shape, in_specs=[SM] * scalars + [VM]...  28.7 us
    all_to_all x1, blocking collectives, per_device(): lax.all_to_all(buffer, ('zh', 'yh'), split_axis=0, concat_axis=0, tiled=T...  25.4 us
    ppermute x10, waiting for transfers between devices, swap_y(): return lax.ppermute(v, 'yl', SWAP)  24.2 us
    all_to_all x1, blocking collectives, per_device(): lax.all_to_all(result, ('zh', 'yh'), split_axis=0, concat_axis=0, tiled=T...  17.7 us
    ppermute x10, starting transfers between devices, swap_y(): return lax.ppermute(v, 'yl', SWAP)  9.67 us
    unnamed x20, local copies, waits for them, and re-layouts  5.58 us
  transfers between devices with their start and end apart: 35, of which 19 were waited for; matrix products, arithmetic and copies ran while one was open for 0% of the time, Pallas kernels for 6%

profile of v2, /device:TPU:32, one launch (start us, length us, event | category | flops | bytes accessed | tf_op | source)
XLA Modules:
  0.0 192.0 jit_solution(231354948525248531)
XLA Ops:
  0.0 0.8 broadcast_select_fusion
  0.8 6.4 %collective-permute-start.2 = (bf16[2,128,128]{2,1,0:T(8,128)(2,1)S(1)}, bf16[2,128,128]{2,1,0:T(8,128)(2,1)S(1)}, u32[]{:S(2)}, u32[]{:S(2)}) collective-permute-start(bf16[2,128,128]{2,1,0:T(8,128)(2,1)S(1)} %get-tuple-element.125), channel_id=1, source_target_pairs={{0,64},{32,96},{64,0},{96,32},{1,65},{33,97},{65,1},{97,33},{2,66}... | collective-permute-start | bytes 196616 | tf_op jit(solution)/shard_map/ppermute | solution.py:298
  7.8 2.4 %collective-permute-start = (bf16[2,128,128]{2,1,0:T(8,128)(2,1)S(1)}, bf16[2,128,128]{2,1,0:T(8,128)(2,1)S(1)}, u32[]{:S(2)}, u32[]{:S(2)}) collective-permute-start(bf16[2,128,128]{2,1,0:T(8,128)(2,1)S(1)} %get-tuple-element.127), channel_id=1, source_target_pairs={{0,32},{32,64},{64,96},{96,0},{1,33},{33,65},{65,97},{97,1},{2,34}... | collective-permute-start | bytes 196616 | tf_op jit(solution)/shard_map/ppermute | solution.py:298
  10.9 1.7 collective-permute-done.1.refs_1_
  12.6 2.1 %collective-permute-done.refs_0_ = bf16[2,128,128]{2,1,0:T(8,128)(2,1)S(1)} collective-permute-done((bf16[2,128,128]{2,1,0:T(8,128)(2,1)S(1)}, bf16[2,128,128]{2,1,0:T(8,128)(2,1)S(1)}, u32[]{:S(2)}, u32[]{:S(2)}) %collective-permute-start) | collective-permute-done | bytes 65568 | tf_op jit(solution)/shard_map/ppermute | solution.py:298
  14.7 0.8 copy-done.2
  15.5 0.8 copy-done.3
  16.3 0.8 copy-done.4
  18.1 3.3 %collective-permute-start.5 = (bf16[2,640,128]{2,1,0:T(8,128)(2,1)S(1)}, bf16[2,640,128]{2,1,0:T(8,128)(2,1)S(1)}, u32[]{:S(2)}, u32[]{:S(2)}) collective-permute-start(bf16[2,640,128]{2,1,0:T(8,128)(2,1)S(1)} %pack_kv.1.refs_0_), channel_id=1, source_target_pairs={{0,16},{8,24},{16,0},{24,8},{1,17},{9,25},{17,1},{25,9},{2,18},{10... | collective-permute-start | bytes 983048 | tf_op jit(solution)/shard_map/ppermute | solution.py:298
  21.4 1.1 collective-permute-start.4
  22.4 1.0 collective-permute-start.3
  23.4 6.8 %collective-permute-done.5.refs_6_ = bf16[2,640,128]{2,1,0:T(8,128)(2,1)S(1)} collective-permute-done((bf16[2,640,128]{2,1,0:T(8,128)(2,1)S(1)}, bf16[2,640,128]{2,1,0:T(8,128)(2,1)S(1)}, u32[]{:S(2)}, u32[]{:S(2)}) %collective-permute-start.5) | collective-permute-done | bytes 327712 | tf_op jit(solution)/shard_map/ppermute | solution.py:298
  30.2 6.9 %collective-permute-done.4.refs_4_ = bf16[2,640,128]{2,1,0:T(8,128)(2,1)S(1)} collective-permute-done((bf16[2,640,128]{2,1,0:T(8,128)(2,1)S(1)}, bf16[2,640,128]{2,1,0:T(8,128)(2,1)S(1)}, u32[]{:S(2)}, u32[]{:S(2)}) %collective-permute-start.4) | collective-permute-done | bytes 327712 | tf_op jit(solution)/shard_map/ppermute | solution.py:298
  37.6 1.1 collective-permute-done.7.refs_3_
  40.4 0.9 copy-done
  41.3 0.9 copy-done.1
  43.0 10.2 %attend.1 = (bf16[128,768]{1,0:T(8,128)(2,1)S(1)}, bf16[8,36,768]{2,1,0:T(8,128)(2,1)S(1)}) custom-call(s32[4]{0:T(128)S(1)} %pad_add_fusion.where_ref, s32[2,128]{1,0:T(2,128)S(1)} %bitcast.19, bf16[2,640,128]{2,1,0:T(8,128)(2,1)S(1)} %pack_kv.1.refs_0_, bf16[2,640,128]{2,1,0:T(8,128)(2,1)S(1)} %collective-permute-done.6.refs_1_, ...), custom_call_target="tpu_custom_call" | custom-call | tf_op jit(solution)/shard_map/attend/pallas_call | solution.py:31
  53.2 1.5 collective-permute-done.12.refs_17_
  54.7 25.4 %all_to_all.10.in_ref = bf16[8,36,768]{2,1,0:T(8,128)(2,1)S(1)} all-to-all(bf16[8,36,768]{2,1,0:T(8,128)(2,1)S(1)} %get-tuple-element.80), channel_id=1, replica_groups=mesh['dp'=2,'zh'=4,'yh'=2,'yl'=2,'core'=2,'x'=4] {'zh','yh'}, dimensions={0} | all-to-all | bytes 884736 | tf_op jit(solution)/shard_map/all_to_all | solution.py:347
  80.1 0.8 collective-permute-start.17
  80.9 1.3 collective-permute-start.16
  82.2 3.0 %collective-permute-start.15 = (bf16[288,384]{1,0:T(8,128)(2,1)S(1)}, bf16[288,384]{1,0:T(8,128)(2,1)S(1)}, u32[]{:S(2)}, u32[]{:S(2)}) collective-permute-start(bf16[288,384]{1,0:T(8,128)(2,1)S(1)} %get-tuple-element.81.refs_0_), channel_id=1, source_target_pairs={{0,2},{1,3},{2,0},{3,1},{4,6},{5,7},{6,4},{7,5},{8,10},{9,11},{10,... | collective-permute-start | bytes 663560 | tf_op jit(solution)/shard_map/ppermute | solution.py:298
  85.2 1.1 collective-permute-start.14
  86.4 0.9 collective-permute-start.13
  87.3 1.2 collective-permute-done.17
  88.5 3.6 %collective-permute-done.16.refs_4_ = bf16[288,384]{1,0:T(8,128)(2,1)S(1)} collective-permute-done((bf16[288,384]{1,0:T(8,128)(2,1)S(1)}, bf16[288,384]{1,0:T(8,128)(2,1)S(1)}, u32[]{:S(2)}, u32[]{:S(2)}) %collective-permute-start.16) | collective-permute-done | bytes 221216 | tf_op jit(solution)/shard_map/ppermute | solution.py:302
  92.1 3.1 %collective-permute-done.14.refs_2_ = bf16[288,384]{1,0:T(8,128)(2,1)S(1)} collective-permute-done((bf16[288,384]{1,0:T(8,128)(2,1)S(1)}, bf16[288,384]{1,0:T(8,128)(2,1)S(1)}, u32[]{:S(2)}, u32[]{:S(2)}) %collective-permute-start.14) | collective-permute-done | bytes 221216 | tf_op jit(solution)/shard_map/ppermute | solution.py:298
  96.0 3.0 %collective-permute-start.20 = (bf16[2,288,384]{2,1,0:T(8,128)(2,1)S(1)}, bf16[2,288,384]{2,1,0:T(8,128)(2,1)S(1)}, u32[]{:S(2)}, u32[]{:S(2)}) collective-permute-start(bf16[2,288,384]{2,1,0:T(8,128)(2,1)S(1)} %pad_maximum_fusion.refs_8_), channel_id=1, source_target_pairs={{0,2},{1,3},{2,0},{3,1},{4,6},{5,7},{6,4},{7,5},{8,10},{9,11},{10,... | collective-permute-start | bytes 1327112 | tf_op jit(solution)/shard_map/ppermute | solution.py:298
  99.0 1.2 collective-permute-start.19
  100.2 0.8 collective-permute-start.18
  101.0 1.3 collective-permute-start.22
  103.0 6.3 %collective-permute-done.22.refs_6_ = bf16[288,384]{1,0:T(8,128)(2,1)S(1)} collective-permute-done((bf16[288,384]{1,0:T(8,128)(2,1)S(1)}, bf16[288,384]{1,0:T(8,128)(2,1)S(1)}, u32[]{:S(2)}, u32[]{:S(2)}) %collective-permute-start.22) | collective-permute-done | bytes 221216 | tf_op jit(solution)/shard_map/ppermute | solution.py:302
  109.4 2.6 %collective-permute-done.23.refs_7_ = bf16[288,384]{1,0:T(8,128)(2,1)S(1)} collective-permute-done((bf16[288,384]{1,0:T(8,128)(2,1)S(1)}, bf16[288,384]{1,0:T(8,128)(2,1)S(1)}, u32[]{:S(2)}, u32[]{:S(2)}) %collective-permute-start.23) | collective-permute-done | bytes 221216 | tf_op jit(solution)/shard_map/ppermute | solution.py:302
  112.0 6.9 %collective-permute-done.19.refs_10_ = bf16[2,288,384]{2,1,0:T(8,128)(2,1)S(1)} collective-permute-done((bf16[2,288,384]{2,1,0:T(8,128)(2,1)S(1)}, bf16[2,288,384]{2,1,0:T(8,128)(2,1)S(1)}, u32[]{:S(2)}, u32[]{:S(2)}) %collective-permute-start.19) | collective-permute-done | bytes 442400 | tf_op jit(solution)/shard_map/ppermute | solution.py:298
  118.9 16.0 %experts.1 = (bf16[288,384]{1,0:T(8,128)(2,1)S(1)}, bf16[288,384]{1,0:T(8,128)(2,1)S(1)}, bf16[288,384]{1,0:T(8,128)(2,1)S(1)}, bf16[288,384]{1,0:T(8,128)(2,1)S...) custom-call(s32[4]{0:T(128)S(1)} %pad_add_fusion.where_ref, ...), custom_call_target="tpu_custom_call" | custom-call | tf_op jit(solution)/shard_map/experts/pallas_call | solution.py:31
  134.9 1.4 collective-permute-start.27
  136.3 1.4 collective-permute-start.24
  137.7 1.8 collective-permute-start.25
  139.5 1.7 collective-permute-start.26
  141.9 1.4 collective-permute-start.29
  143.3 6.3 %collective-permute-done.28.refs_4_ = bf16[288,384]{1,0:T(8,128)(2,1)S(1)} collective-permute-done((bf16[288,384]{1,0:T(8,128)(2,1)S(1)}, bf16[288,384]{1,0:T(8,128)(2,1)S(1)}, u32[]{:S(2)}, u32[]{:S(2)}) %collective-permute-start.28) | collective-permute-done | bytes 221216 | tf_op jit(solution)/shard_map/ppermute | solution.py:302
  150.3 4.0 %collective-permute-done.29.refs_5_ = bf16[288,384]{1,0:T(8,128)(2,1)S(1)} collective-permute-done((bf16[288,384]{1,0:T(8,128)(2,1)S(1)}, bf16[288,384]{1,0:T(8,128)(2,1)S(1)}, u32[]{:S(2)}, u32[]{:S(2)}) %collective-permute-start.29) | collective-permute-done | bytes 221216 | tf_op jit(solution)/shard_map/ppermute | solution.py:302
  154.3 5.3 %collective-permute-done.26.refs_9_ = bf16[2,288,384]{2,1,0:T(8,128)(2,1)S(1)} collective-permute-done((bf16[2,288,384]{2,1,0:T(8,128)(2,1)S(1)}, bf16[2,288,384]{2,1,0:T(8,128)(2,1)S(1)}, u32[]{:S(2)}, u32[]{:S(2)}) %collective-permute-start.26) | collective-permute-done | bytes 442400 | tf_op jit(solution)/shard_map/ppermute | solution.py:298
  160.1 1.2 collective-permute-start.30
  161.3 2.1 %collective-permute-start.31 = (bf16[288,384]{1,0:T(8,128)(2,1)S(1)}, bf16[288,384]{1,0:T(8,128)(2,1)S(1)}, u32[]{:S(2)}, u32[]{:S(2)}) collective-permute-start(bf16[288,384]{1,0:T(8,128)(2,1)S(1)} %get-tuple-element.115), channel_id=1, source_target_pairs={{0,3},{1,0},{2,1},{3,2},{4,7},{5,4},{6,5},{7,6},{8,11},{9,8},{10,9... | collective-permute-start | bytes 663560 | tf_op jit(solution)/shard_map/ppermute | solution.py:298
  164.1 8.1 %collective-permute-done.30.refs_1_ = bf16[288,384]{1,0:T(8,128)(2,1)S(1)} collective-permute-done((bf16[288,384]{1,0:T(8,128)(2,1)S(1)}, bf16[288,384]{1,0:T(8,128)(2,1)S(1)}, u32[]{:S(2)}, u32[]{:S(2)}) %collective-permute-start.30) | collective-permute-done | bytes 221216 | tf_op jit(solution)/shard_map/ppermute | solution.py:298
  172.5 17.7 %all_to_all.11.part_ref = bf16[8,36,768]{2,1,0:T(8,128)(2,1)S(1)} all-to-all(bf16[8,36,768]{2,1,0:T(8,128)(2,1)S(1)} %last_sum.1), channel_id=1, replica_groups=mesh['dp'=2,'zh'=4,'yh'=2,'yl'=2,'core'=2,'x'=4] {'zh','yh'}, dimensions={0} | all-to-all | bytes 884736 | tf_op jit(solution)/shard_map/all_to_all | solution.py:382
  190.3 1.7 mix.1
  (54 shorter events, 9.5 us)
Async XLA Ops:
  0.0 118.9 %copy-start.6 = (f32[3072]{0:T(1024)S(1)}, f32[3072]{0:T(1024)}, u32[]{:S(2)}) copy-start(f32[3072]{0:T(1024)} %param.18) | copy-start | bytes 36868
  0.8 10.0 %collective-permute-start.2 = (bf16[2,128,128]{2,1,0:T(8,128)(2,1)S(1)}, bf16[2,128,128]{2,1,0:T(8,128)(2,1)S(1)}, u32[]{:S(2)}, u32[]{:S(2)}) collective-permute-start(bf16[2,128,128]{2,1,0:T(8,128)(2,1)S(1)} %get-tuple-element.125), channel_id=1, source_target_pairs={{0,64},{32,96},{64,0},{96,32},{1,65},{33,97},{65,1},{97,33},{2,66}... | collective-permute-start | bytes 196616 | tf_op jit(solution)/shard_map/ppermute | solution.py:298
  7.2 5.4 %collective-permute-start.1 = (bf16[2,128,128]{2,1,0:T(8,128)(2,1)S(1)}, bf16[2,128,128]{2,1,0:T(8,128)(2,1)S(1)}, u32[]{:S(2)}, u32[]{:S(2)}) collective-permute-start(bf16[2,128,128]{2,1,0:T(8,128)(2,1)S(1)} %get-tuple-element.126), channel_id=1, source_target_pairs={{0,96},{32,0},{64,32},{96,64},{1,97},{33,1},{65,33},{97,65},{2,98}... | collective-permute-start | bytes 196616 | tf_op jit(solution)/shard_map/ppermute | solution.py:298
  7.8 7.0 %collective-permute-start = (bf16[2,128,128]{2,1,0:T(8,128)(2,1)S(1)}, bf16[2,128,128]{2,1,0:T(8,128)(2,1)S(1)}, u32[]{:S(2)}, u32[]{:S(2)}) collective-permute-start(bf16[2,128,128]{2,1,0:T(8,128)(2,1)S(1)} %get-tuple-element.127), channel_id=1, source_target_pairs={{0,32},{32,64},{64,96},{96,0},{1,33},{33,65},{65,97},{97,1},{2,34}... | collective-permute-start | bytes 196616 | tf_op jit(solution)/shard_map/ppermute | solution.py:298
  14.7 0.8 copy-start.2
  15.5 0.8 copy-start.3
  16.3 0.8 copy-start.4
  17.0 0.8 copy-start.5
  18.0 5.4 %collective-permute-start.6 = (bf16[2,640,128]{2,1,0:T(8,128)(2,1)S(1)}, bf16[2,640,128]{2,1,0:T(8,128)(2,1)S(1)}, u32[]{:S(2)}, u32[]{:S(2)}) collective-permute-start(bf16[2,640,128]{2,1,0:T(8,128)(2,1)S(1)} %pack_kv.1.refs_0_), channel_id=1, source_target_pairs={{0,4},{4,0},{1,5},{5,1},{2,6},{6,2},{3,7},{7,3},{8,12},{12,8},{9,1... | collective-permute-start | bytes 983048 | tf_op jit(solution)/shard_map/ppermute | solution.py:306
  18.1 12.2 %collective-permute-start.5 = (bf16[2,640,128]{2,1,0:T(8,128)(2,1)S(1)}, bf16[2,640,128]{2,1,0:T(8,128)(2,1)S(1)}, u32[]{:S(2)}, u32[]{:S(2)}) collective-permute-start(bf16[2,640,128]{2,1,0:T(8,128)(2,1)S(1)} %pack_kv.1.refs_0_), channel_id=1, source_target_pairs={{0,16},{8,24},{16,0},{24,8},{1,17},{9,25},{17,1},{25,9},{2,18},{10... | collective-permute-start | bytes 983048 | tf_op jit(solution)/shard_map/ppermute | solution.py:298
  21.4 15.8 %collective-permute-start.4 = (bf16[2,640,128]{2,1,0:T(8,128)(2,1)S(1)}, bf16[2,640,128]{2,1,0:T(8,128)(2,1)S(1)}, u32[]{:S(2)}, u32[]{:S(2)}) collective-permute-start(bf16[2,640,128]{2,1,0:T(8,128)(2,1)S(1)} %pack_kv.1.refs_0_), channel_id=1, source_target_pairs={{0,24},{8,0},{16,8},{24,16},{1,25},{9,1},{17,9},{25,17},{2,26},{10... | collective-permute-start | bytes 983048 | tf_op jit(solution)/shard_map/ppermute | solution.py:298
  22.4 14.7 %collective-permute-start.3 = (bf16[2,640,128]{2,1,0:T(8,128)(2,1)S(1)}, bf16[2,640,128]{2,1,0:T(8,128)(2,1)S(1)}, u32[]{:S(2)}, u32[]{:S(2)}) collective-permute-start(bf16[2,640,128]{2,1,0:T(8,128)(2,1)S(1)} %pack_kv.1.refs_0_), channel_id=1, source_target_pairs={{0,8},{8,16},{16,24},{24,0},{1,9},{9,17},{17,25},{25,1},{2,10},{10... | collective-permute-start | bytes 983048 | tf_op jit(solution)/shard_map/ppermute | solution.py:298
  37.1 1.6 collective-permute-start.7
  37.1 2.1 %collective-permute-start.8 = (bf16[2,640,128]{2,1,0:T(8,128)(2,1)S(1)}, bf16[2,640,128]{2,1,0:T(8,128)(2,1)S(1)}, u32[]{:S(2)}, u32[]{:S(2)}) collective-permute-start(bf16[2,640,128]{2,1,0:T(8,128)(2,1)S(1)} %collective-permute-done.4.refs_4_), channel_id=1, source_target_pairs={{0,4},{4,0},{1,5},{5,1},{2,6},{6,2},{3,7},{7,3},{8,12},{12,8},{9,1... | collective-permute-start | bytes 983048 | tf_op jit(solution)/shard_map/ppermute | solution.py:306
  37.6 2.1 %collective-permute-start.9 = (bf16[2,640,128]{2,1,0:T(8,128)(2,1)S(1)}, bf16[2,640,128]{2,1,0:T(8,128)(2,1)S(1)}, u32[]{:S(2)}, u32[]{:S(2)}) collective-permute-start(bf16[2,640,128]{2,1,0:T(8,128)(2,1)S(1)} %collective-permute-done.5.refs_6_), channel_id=1, source_target_pairs={{0,4},{4,0},{1,5},{5,1},{2,6},{6,2},{3,7},{7,3},{8,12},{12,8},{9,1... | collective-permute-start | bytes 983048 | tf_op jit(solution)/shard_map/ppermute | solution.py:306
  39.7 13.5 %collective-permute-start.10 = (bf16[3072,512]{1,0:T(8,128)(2,1)}, bf16[3072,512]{1,0:T(8,128)(2,1)}, u32[]{:S(2)}, u32[]{:S(2)}) collective-permute-start(bf16[3072,512]{1,0:T(8,128)(2,1)} %refs_12_.1), channel_id=1, source_target_pairs={{0,4},{4,0},{1,5},{5,1},{2,6},{6,2},{3,7},{7,3},{8,12},{12,8},{9,1... | collective-permute-start | bytes 9437192 | tf_op jit(solution)/shard_map/ppermute | solution.py:306
  39.8 13.3 %collective-permute-start.11 = (bf16[3072,512]{1,0:T(8,128)(2,1)}, bf16[3072,512]{1,0:T(8,128)(2,1)}, u32[]{:S(2)}, u32[]{:S(2)}) collective-permute-start(bf16[3072,512]{1,0:T(8,128)(2,1)} %refs_13_.1), channel_id=1, source_target_pairs={{0,4},{4,0},{1,5},{5,1},{2,6},{6,2},{3,7},{7,3},{8,12},{12,8},{9,1... | collective-permute-start | bytes 9437192 | tf_op jit(solution)/shard_map/ppermute | solution.py:306
  40.2 14.5 %collective-permute-start.12 = (bf16[512,3072]{1,0:T(8,128)(2,1)}, bf16[512,3072]{1,0:T(8,128)(2,1)}, u32[]{:S(2)}, u32[]{:S(2)}) collective-permute-start(bf16[512,3072]{1,0:T(8,128)(2,1)} %refs_14_.1), channel_id=1, source_target_pairs={{0,4},{4,0},{1,5},{5,1},{2,6},{6,2},{3,7},{7,3},{8,12},{12,8},{9,1... | collective-permute-start | bytes 9437192 | tf_op jit(solution)/shard_map/ppermute | solution.py:306
  40.4 0.9 copy-start
  41.3 0.9 copy-start.1
  42.3 0.7 copy-start.7
  80.1 8.4 %collective-permute-start.17 = (bf16[288,384]{1,0:T(8,128)(2,1)S(1)}, bf16[288,384]{1,0:T(8,128)(2,1)S(1)}, u32[]{:S(2)}, u32[]{:S(2)}) collective-permute-start(bf16[288,384]{1,0:T(8,128)(2,1)S(1)} %get-tuple-element.82), channel_id=1, source_target_pairs={{0,8},{8,0},{1,9},{9,1},{2,10},{10,2},{3,11},{11,3},{4,12},{12,4},... | collective-permute-start | bytes 663560 | tf_op jit(solution)/shard_map/ppermute | solution.py:302
  80.9 11.3 %collective-permute-start.16 = (bf16[288,384]{1,0:T(8,128)(2,1)S(1)}, bf16[288,384]{1,0:T(8,128)(2,1)S(1)}, u32[]{:S(2)}, u32[]{:S(2)}) collective-permute-start(bf16[288,384]{1,0:T(8,128)(2,1)S(1)} %get-tuple-element.81.refs_0_), channel_id=1, source_target_pairs={{0,8},{8,0},{1,9},{9,1},{2,10},{10,2},{3,11},{11,3},{4,12},{12,4},... | collective-permute-start | bytes 663560 | tf_op jit(solution)/shard_map/ppermute | solution.py:302
  82.2 9.9 %collective-permute-start.15 = (bf16[288,384]{1,0:T(8,128)(2,1)S(1)}, bf16[288,384]{1,0:T(8,128)(2,1)S(1)}, u32[]{:S(2)}, u32[]{:S(2)}) collective-permute-start(bf16[288,384]{1,0:T(8,128)(2,1)S(1)} %get-tuple-element.81.refs_0_), channel_id=1, source_target_pairs={{0,2},{1,3},{2,0},{3,1},{4,6},{5,7},{6,4},{7,5},{8,10},{9,11},{10,... | collective-permute-start | bytes 663560 | tf_op jit(solution)/shard_map/ppermute | solution.py:298
  85.2 10.0 %collective-permute-start.14 = (bf16[288,384]{1,0:T(8,128)(2,1)S(1)}, bf16[288,384]{1,0:T(8,128)(2,1)S(1)}, u32[]{:S(2)}, u32[]{:S(2)}) collective-permute-start(bf16[288,384]{1,0:T(8,128)(2,1)S(1)} %get-tuple-element.81.refs_0_), channel_id=1, source_target_pairs={{0,3},{1,0},{2,1},{3,2},{4,7},{5,4},{6,5},{7,6},{8,11},{9,8},{10,9... | collective-permute-start | bytes 663560 | tf_op jit(solution)/shard_map/ppermute | solution.py:298
  86.4 8.9 %collective-permute-start.13 = (bf16[288,384]{1,0:T(8,128)(2,1)S(1)}, bf16[288,384]{1,0:T(8,128)(2,1)S(1)}, u32[]{:S(2)}, u32[]{:S(2)}) collective-permute-start(bf16[288,384]{1,0:T(8,128)(2,1)S(1)} %get-tuple-element.81.refs_0_), channel_id=1, source_target_pairs={{0,1},{1,2},{2,3},{3,0},{4,5},{5,6},{6,7},{7,4},{8,9},{9,10},{10,1... | collective-permute-start | bytes 663560 | tf_op jit(solution)/shard_map/ppermute | solution.py:298
  95.3 7.1 %collective-permute-start.21 = (bf16[288,384]{1,0:T(8,128)(2,1)S(1)}, bf16[288,384]{1,0:T(8,128)(2,1)S(1)}, u32[]{:S(2)}, u32[]{:S(2)}) collective-permute-start(bf16[288,384]{1,0:T(8,128)(2,1)S(1)} %collective-permute-done.13.refs_1_), channel_id=1, source_target_pairs={{0,8},{8,0},{1,9},{9,1},{2,10},{10,2},{3,11},{11,3},{4,12},{12,4},... | collective-permute-start | bytes 663560 | tf_op jit(solution)/shard_map/ppermute | solution.py:302
  96.0 16.0 %collective-permute-start.20 = (bf16[2,288,384]{2,1,0:T(8,128)(2,1)S(1)}, bf16[2,288,384]{2,1,0:T(8,128)(2,1)S(1)}, u32[]{:S(2)}, u32[]{:S(2)}) collective-permute-start(bf16[2,288,384]{2,1,0:T(8,128)(2,1)S(1)} %pad_maximum_fusion.refs_8_), channel_id=1, source_target_pairs={{0,2},{1,3},{2,0},{3,1},{4,6},{5,7},{6,4},{7,5},{8,10},{9,11},{10,... | collective-permute-start | bytes 1327112 | tf_op jit(solution)/shard_map/ppermute | solution.py:298
  99.0 19.9 %collective-permute-start.19 = (bf16[2,288,384]{2,1,0:T(8,128)(2,1)S(1)}, bf16[2,288,384]{2,1,0:T(8,128)(2,1)S(1)}, u32[]{:S(2)}, u32[]{:S(2)}) collective-permute-start(bf16[2,288,384]{2,1,0:T(8,128)(2,1)S(1)} %pad_maximum_fusion.refs_8_), channel_id=1, source_target_pairs={{0,3},{1,0},{2,1},{3,2},{4,7},{5,4},{6,5},{7,6},{8,11},{9,8},{10,9... | collective-permute-start | bytes 1327112 | tf_op jit(solution)/shard_map/ppermute | solution.py:298
  100.2 18.7 %collective-permute-start.18 = (bf16[2,288,384]{2,1,0:T(8,128)(2,1)S(1)}, bf16[2,288,384]{2,1,0:T(8,128)(2,1)S(1)}, u32[]{:S(2)}, u32[]{:S(2)}) collective-permute-start(bf16[2,288,384]{2,1,0:T(8,128)(2,1)S(1)} %pad_maximum_fusion.refs_8_), channel_id=1, source_target_pairs={{0,1},{1,2},{2,3},{3,0},{4,5},{5,6},{6,7},{7,4},{8,9},{9,10},{10,1... | collective-permute-start | bytes 1327112 | tf_op jit(solution)/shard_map/ppermute | solution.py:298
  101.0 8.4 %collective-permute-start.22 = (bf16[288,384]{1,0:T(8,128)(2,1)S(1)}, bf16[288,384]{1,0:T(8,128)(2,1)S(1)}, u32[]{:S(2)}, u32[]{:S(2)}) collective-permute-start(bf16[288,384]{1,0:T(8,128)(2,1)S(1)} %collective-permute-done.14.refs_2_), channel_id=1, source_target_pairs={{0,8},{8,0},{1,9},{9,1},{2,10},{10,2},{3,11},{11,3},{4,12},{12,4},... | collective-permute-start | bytes 663560 | tf_op jit(solution)/shard_map/ppermute | solution.py:302
  102.3 9.6 %collective-permute-start.23 = (bf16[288,384]{1,0:T(8,128)(2,1)S(1)}, bf16[288,384]{1,0:T(8,128)(2,1)S(1)}, u32[]{:S(2)}, u32[]{:S(2)}) collective-permute-start(bf16[288,384]{1,0:T(8,128)(2,1)S(1)} %collective-permute-done.15.refs_3_), channel_id=1, source_target_pairs={{0,8},{8,0},{1,9},{9,1},{2,10},{10,2},{3,11},{11,3},{4,12},{12,4},... | collective-permute-start | bytes 663560 | tf_op jit(solution)/shard_map/ppermute | solution.py:302
  134.8 55.4 %copy-start.8 = (s32[128,2]{0,1:T(2,128)S(1)}, s32[128,2]{0,1:T(2,128)}, u32[]{:S(2)}) copy-start(s32[128,2]{0,1:T(2,128)} %param.22) | copy-start | bytes 3076
  134.9 55.4 %copy-start.9 = (f32[128,2]{0,1:T(2,128)S(1)}, f32[128,2]{0,1:T(2,128)}, u32[]{:S(2)}) copy-start(f32[128,2]{0,1:T(2,128)} %param.23) | copy-start | bytes 3076
  134.9 7.1 %collective-permute-start.27 = (bf16[288,384]{1,0:T(8,128)(2,1)S(1)}, bf16[288,384]{1,0:T(8,128)(2,1)S(1)}, u32[]{:S(2)}, u32[]{:S(2)}) collective-permute-start(bf16[288,384]{1,0:T(8,128)(2,1)S(1)} %get-tuple-element.104), channel_id=1, source_target_pairs={{0,8},{8,0},{1,9},{9,1},{2,10},{10,2},{3,11},{11,3},{4,12},{12,4},... | collective-permute-start | bytes 663560 | tf_op jit(solution)/shard_map/ppermute | solution.py:302
  136.3 18.0 %collective-permute-start.24 = (bf16[2,288,384]{2,1,0:T(8,128)(2,1)S(1)}, bf16[2,288,384]{2,1,0:T(8,128)(2,1)S(1)}, u32[]{:S(2)}, u32[]{:S(2)}) collective-permute-start(bf16[2,288,384]{2,1,0:T(8,128)(2,1)S(1)} %get-tuple-element.101), channel_id=1, source_target_pairs={{0,1},{1,2},{2,3},{3,0},{4,5},{5,6},{6,7},{7,4},{8,9},{9,10},{10,1... | collective-permute-start | bytes 1327112 | tf_op jit(solution)/shard_map/ppermute | solution.py:298
  137.7 16.6 %collective-permute-start.25 = (bf16[2,288,384]{2,1,0:T(8,128)(2,1)S(1)}, bf16[2,288,384]{2,1,0:T(8,128)(2,1)S(1)}, u32[]{:S(2)}, u32[]{:S(2)}) collective-permute-start(bf16[2,288,384]{2,1,0:T(8,128)(2,1)S(1)} %get-tuple-element.102), channel_id=1, source_target_pairs={{0,3},{1,0},{2,1},{3,2},{4,7},{5,4},{6,5},{7,6},{8,11},{9,8},{10,9... | collective-permute-start | bytes 1327112 | tf_op jit(solution)/shard_map/ppermute | solution.py:298
  139.5 20.1 %collective-permute-start.26 = (bf16[2,288,384]{2,1,0:T(8,128)(2,1)S(1)}, bf16[2,288,384]{2,1,0:T(8,128)(2,1)S(1)}, u32[]{:S(2)}, u32[]{:S(2)}) collective-permute-start(bf16[2,288,384]{2,1,0:T(8,128)(2,1)S(1)} %get-tuple-element.103), channel_id=1, source_target_pairs={{0,2},{1,3},{2,0},{3,1},{4,6},{5,7},{6,4},{7,5},{8,10},{9,11},{10,... | collective-permute-start | bytes 1327112 | tf_op jit(solution)/shard_map/ppermute | solution.py:298
  141.2 8.4 %collective-permute-start.28 = (bf16[288,384]{1,0:T(8,128)(2,1)S(1)}, bf16[288,384]{1,0:T(8,128)(2,1)S(1)}, u32[]{:S(2)}, u32[]{:S(2)}) collective-permute-start(bf16[288,384]{1,0:T(8,128)(2,1)S(1)} %get-tuple-element.105), channel_id=1, source_target_pairs={{0,8},{8,0},{1,9},{9,1},{2,10},{10,2},{3,11},{11,3},{4,12},{12,4},... | collective-permute-start | bytes 663560 | tf_op jit(solution)/shard_map/ppermute | solution.py:302
  141.9 12.4 %collective-permute-start.29 = (bf16[288,384]{1,0:T(8,128)(2,1)S(1)}, bf16[288,384]{1,0:T(8,128)(2,1)S(1)}, u32[]{:S(2)}, u32[]{:S(2)}) collective-permute-start(bf16[288,384]{1,0:T(8,128)(2,1)S(1)} %get-tuple-element.106), channel_id=1, source_target_pairs={{0,8},{8,0},{1,9},{9,1},{2,10},{10,2},{3,11},{11,3},{4,12},{12,4},... | collective-permute-start | bytes 663560 | tf_op jit(solution)/shard_map/ppermute | solution.py:302
  149.6 14.5 %collective-permute-start.33 = (bf16[288,384]{1,0:T(8,128)(2,1)S(1)}, bf16[288,384]{1,0:T(8,128)(2,1)S(1)}, u32[]{:S(2)}, u32[]{:S(2)}) collective-permute-start(bf16[288,384]{1,0:T(8,128)(2,1)S(1)} %get-tuple-element.117), channel_id=1, source_target_pairs={{0,8},{8,0},{1,9},{9,1},{2,10},{10,2},{3,11},{11,3},{4,12},{12,4},... | collective-permute-start | bytes 663560 | tf_op jit(solution)/shard_map/ppermute | solution.py:302
  160.1 12.2 %collective-permute-start.30 = (bf16[288,384]{1,0:T(8,128)(2,1)S(1)}, bf16[288,384]{1,0:T(8,128)(2,1)S(1)}, u32[]{:S(2)}, u32[]{:S(2)}) collective-permute-start(bf16[288,384]{1,0:T(8,128)(2,1)S(1)} %get-tuple-element.114), channel_id=1, source_target_pairs={{0,1},{1,2},{2,3},{3,0},{4,5},{5,6},{6,7},{7,4},{8,9},{9,10},{10,1... | collective-permute-start | bytes 663560 | tf_op jit(solution)/shard_map/ppermute | solution.py:298
  161.3 11.0 %collective-permute-start.31 = (bf16[288,384]{1,0:T(8,128)(2,1)S(1)}, bf16[288,384]{1,0:T(8,128)(2,1)S(1)}, u32[]{:S(2)}, u32[]{:S(2)}) collective-permute-start(bf16[288,384]{1,0:T(8,128)(2,1)S(1)} %get-tuple-element.115), channel_id=1, source_target_pairs={{0,3},{1,0},{2,1},{3,2},{4,7},{5,4},{6,5},{7,6},{8,11},{9,8},{10,9... | collective-permute-start | bytes 663560 | tf_op jit(solution)/shard_map/ppermute | solution.py:298
  163.4 8.9 %collective-permute-start.32 = (bf16[288,384]{1,0:T(8,128)(2,1)S(1)}, bf16[288,384]{1,0:T(8,128)(2,1)S(1)}, u32[]{:S(2)}, u32[]{:S(2)}) collective-permute-start(bf16[288,384]{1,0:T(8,128)(2,1)S(1)} %get-tuple-element.116), channel_id=1, source_target_pairs={{0,2},{1,3},{2,0},{3,1},{4,6},{5,7},{6,4},{7,5},{8,10},{9,11},{10,... | collective-permute-start | bytes 663560 | tf_op jit(solution)/shard_map/ppermute | solution.py:298
  163.4 8.8 %collective-permute-start.34 = (bf16[288,384]{1,0:T(8,128)(2,1)S(1)}, bf16[288,384]{1,0:T(8,128)(2,1)S(1)}, u32[]{:S(2)}, u32[]{:S(2)}) collective-permute-start(bf16[288,384]{1,0:T(8,128)(2,1)S(1)} %get-tuple-element.118), channel_id=1, source_target_pairs={{0,8},{8,0},{1,9},{9,1},{2,10},{10,2},{3,11},{11,3},{4,12},{12,4},... | collective-permute-start | bytes 663560 | tf_op jit(solution)/shard_map/ppermute | solution.py:302
